TPU v7x, 32 devices: a whole 2x2x4 slice. The times are simulated.
32 devices in a mesh: group: 2 (over y), gz: 4 (over z), gy: 2 (over x), gx: 2 (over core).
Axes of the slice: x: 2, y: 2, z: 4, core: 2. Of those that a mesh axis runs over, the one named last changes fastest.
Arguments:
- volume: bfloat16 [32, 32, 16, 512], P(None, ('group', 'gz'), 'gy', 'gx'), parts along dimension 1, may hold values from -6 to 6
- first_weight: bfloat16 [3, 3, 3, 32, 32], replicated, may hold values from -0.21875 to 0.21875
- second_weight: bfloat16 [3, 3, 3, 32, 32], replicated, may hold values from -0.21875 to 0.21875
- sample_index: int32 [8, 2, 2, 256], P(('group', 'gz'), 'gy', 'gx'), parts along dimension 0, may hold values from 0 to 8191
- segments: int32 [8, 2, 2, 256], P('group', 'gy', 'gx'), parts along dimension 0, may hold values from 0 to 63
- block_match: int32 [8, 4], P('group'), parts along dimension 0, may hold values from 0 to 1, as said below
Outputs:
- features: bfloat16 [32, 32, 16, 512], P(None, ('group', 'gz'), 'gy', 'gx'), parts along dimension 1
- row_loss: float32 [8, 2, 2, 256], P(('group', 'gz'), 'gy', 'gx'), parts along dimension 0
There are 2 independent parts, one for each index of `group`. A program takes and returns all parts, laid end to end along the dimension named above; an argument that names none is the same for every part. Nothing has to cross between parts.
Inputs may be any that keep to these rules, and one draw needn't show every extreme that they name: `sample_index`: the voxel of a row is z * 8 * 256 + y * 256 + x in its block's local coordinates. `block_match`: entry [a, a2] is 1 when block a contrasts against block a2; the diagonal is 1.
All inputs are finite; a program needn't handle non-finite values.
Results may differ from a plain program's by a relative error of at most 0.0034.
Values may be sent and summed in bfloat16 or wider, within the bound.
A program may use at most 128 MiB of HBM per device.

v0:
```python
import jax
import jax.numpy as jnp
from jax import lax
from jax.sharding import PartitionSpec as P

SOFTMAX_WARMTH = 0.25


def extended(shard, sides, width):
    for axis, dim in sides:
        count, length = (lax.axis_size(axis), shard.shape[dim])
        up = [(i, (i + 1) % count) for i in range(count - 1)]
        down = [(j, i) for i, j in up]
        last = lax.slice_in_dim(shard, length - width, length, axis=dim)
        leading = lax.slice_in_dim(shard, 0, width, axis=dim)
        before = lax.ppermute(last, axis, up)
        after = lax.ppermute(leading, axis, down)
        shard = jnp.concatenate([before, shard, after], axis=dim)
    return shard


def conv_valid(padded, weight):
    channels = padded.shape[0]
    out_z = padded.shape[1] - 2
    out_y = padded.shape[2] - 2
    out_x = padded.shape[3] - 2
    outputs = weight.shape[3]
    reduced_total = jnp.zeros((outputs, out_z * out_y * out_x), jnp.float32)
    for offset_z in range(3):
        plane = padded[:, offset_z : offset_z + out_z]
        stacked = jnp.stack(
            [
                plane[:, :, offset_y : offset_y + out_y, column_shift : column_shift + out_x]
                for offset_y in range(3)
                for column_shift in range(3)
            ],
            axis=0,
        )
        patches = stacked.reshape(9 * channels, out_z * out_y * out_x)
        kernel = jnp.transpose(weight[offset_z], (2, 0, 1, 3)).reshape(outputs, 9 * channels)
        reduced_total = reduced_total + jnp.dot(kernel, patches, preferred_element_type=jnp.float32)
    return reduced_total.reshape(outputs, out_z, out_y, out_x)


def pad_layer(activ_in):
    return extended(activ_in, (("gz", 1), ("gy", 2), ("gx", 3)), 1)


def shards(volume, first_weight, second_weight, sample_index, segments, block_match):
    channels, slab_depth, tile_height, tile_width = volume.shape
    hidden = jax.nn.relu(conv_valid(pad_layer(volume), first_weight)).astype(jnp.bfloat16)
    conv_out = conv_valid(pad_layer(hidden), second_weight)
    features = (conv_out + volume.astype(jnp.float32)).astype(jnp.bfloat16)
    flattened = features.reshape(channels, -1)
    picked = jnp.take(flattened, sample_index.reshape(-1), axis=1).astype(jnp.float32)
    embedding = (picked / jnp.sqrt(jnp.sum(picked * picked, axis=0) + 1.0)).astype(jnp.bfloat16)
    query_rows = embedding[None]
    own_block = lax.axis_index("gz")
    seg_all = segments.reshape(segments.shape[0], -1)
    home_segment_label = lax.dynamic_index_in_dim(seg_all, own_block, 0, keepdims=False)
    match_float = block_match.astype(jnp.float32)
    rows = embedding.shape[1]
    match_row = lax.dynamic_index_in_dim(match_float, own_block, 0, keepdims=False)
    similarity_logits = (
        jnp.einsum(
            "cr,kcs->rks",
            embedding,
            lax.all_gather(query_rows, "gz", axis=0, tiled=True),
            preferred_element_type=jnp.float32,
        )
        / SOFTMAX_WARMTH
    )
    same_seg = (home_segment_label[:, None, None] == seg_all[None]).astype(jnp.float32)
    exp_terms = jnp.exp(similarity_logits) * match_row[None, :, None]
    reduced_total = jnp.sum(exp_terms, axis=(1, 2))
    positive = jnp.sum(exp_terms * same_seg, axis=(1, 2))
    row_loss = (jnp.log(reduced_total) - jnp.log(positive)).reshape(1, 1, 1, rows)
    return (features, row_loss)


def solution(mesh):
    in_specs = (
        P(None, ("group", "gz"), "gy", "gx"),
        P(),
        P(),
        P(("group", "gz"), "gy", "gx", None),
        P("group", "gy", "gx", None),
        P("group", None),
    )
    out_specs = (P(None, ("group", "gz"), "gy", "gx"), P(("group", "gz"), "gy", "gx", None))
    return jax.shard_map(shards, mesh=mesh, in_specs=in_specs, out_specs=out_specs, check_vma=False)
```

profile of v0, /device:TPU:0, one launch (start us, length us, event | category | flops | bytes accessed | tf_op | source)
XLA Modules:
  0.0 274.9 jit_solution(13628984462543033317)
XLA Ops:
  1.6 4.9 %collective-permute-start = (bf16[32,1,8,256]{3,2,1,0:T(8,128)(2,1)S(1)}, bf16[32,1,8,256]{3,2,1,0:T(8,128)(2,1)S(1)}, u32[]{:S(2)}, u32[]{:S(2)}) collective-permute-start(bf16[32,1,8,256]{3,2,1,0:T(8,128)(2,1)S(1)} %get-tuple-element.74), channel_id=1, source_target_pairs={{0,4},{4,8},{8,12},{1,5},{5,9},{9,13},{2,6},{6,10},{10,14},{3,7},{... | collective-permute-start | bytes 393224 | tf_op jit(solution)/shard_map/ppermute | solution.py:16
  8.9 1.6 slice_bitcast_fusion
  13.5 3.5 %copy.224 = bf16[32,6,8,256]{0,1,3,2:T(8,128)(2,1)} copy(bf16[32,6,8,256]{3,2,1,0:T(8,128)(2,1)S(1)} %constant_dynamic-update-slice_fusion) | data formatting | bytes 1572864 | tf_op jit(solution)/shard_map/concatenate | solution.py:18
  17.0 2.4 fusion.111
  19.4 3.4 %collective-permute-start.2 = (bf16[32,6,1,256]{0,1,3,2:T(8,128)(2,1)}, bf16[32,6,1,256]{0,1,3,2:T(8,128)(2,1)S(1)}, u32[]{:S(2)}, u32[]{:S(2)}) collective-permute-start(bf16[32,6,1,256]{0,1,3,2:T(8,128)(2,1)} %get-tuple-element.10), channel_id=1, source_target_pairs={{0,2},{1,3},{4,6},{5,7},{8,10},{9,11},{12,14},{13,15},{16,18},{17,... | collective-permute-start | bytes 294920 | tf_op jit(solution)/shard_map/ppermute | solution.py:16
  25.4 7.4 %collective-permute-done.2 = bf16[32,6,1,256]{0,1,3,2:T(8,128)(2,1)S(1)} collective-permute-done((bf16[32,6,1,256]{0,1,3,2:T(8,128)(2,1)}, bf16[32,6,1,256]{0,1,3,2:T(8,128)(2,1)S(1)}, u32[]{:S(2)}, u32[]{:S(2)}) %collective-permute-start.2) | collective-permute-done | bytes 98336 | tf_op jit(solution)/shard_map/ppermute | solution.py:16
  32.8 4.0 %collective-permute-done.3 = bf16[32,6,1,256]{0,1,3,2:T(8,128)(2,1)S(1)} collective-permute-done((bf16[32,6,1,256]{0,1,3,2:T(8,128)(2,1)}, bf16[32,6,1,256]{0,1,3,2:T(8,128)(2,1)S(1)}, u32[]{:S(2)}, u32[]{:S(2)}) %collective-permute-start.3) | collective-permute-done | bytes 98336 | tf_op jit(solution)/shard_map/ppermute | solution.py:17
  36.8 3.8 %pad_maximum_fusion = bf16[32,6,10,256]{0,1,3,2:T(8,128)(2,1)S(1)} fusion(bf16[32,6,1,256]{0,1,3,2:T(8,128)(2,1)S(1)} %collective-permute-done.3, bf16[32,6,8,256]{0,1,3,2:T(8,128)(2,1)} %copy.224, bf16[32,6,1,256]{0,1,3,2:T(8,128)(2,1)S(1)} %collective-permute-done.2), kind=kLoop, calls=%fused_computation.7 | loop fusion | flops 983040 | bytes 1966080 | tf_op jit(solution)/shard_map/concatenate | solution.py:18
  40.7 2.3 copy-done
  44.3 1.8 collective-permute-start.5
  46.7 1.7 fusion.93
  48.4 4.5 %copy.228 = bf16[32,6,10,256]{3,0,2,1:T(8,128)(2,1)S(1)} copy(bf16[32,6,10,256]{0,1,3,2:T(8,128)(2,1)} %copy-done) | data formatting | bytes 1966080 | tf_op jit(solution)/shard_map/concatenate | solution.py:18
  53.4 3.6 %fusion.94 = (bf16[1,32,4,8,256]{4,1,3,2,0:T(8,128)(2,1)}, bf16[1,32,4,8,256]{4,1,3,2,0:T(8,128)(2,1)S(1)}, bf16[1,32,4,8,256]{4,1,3,2,0:T(8,128)(2,1)}, bf16[1,...) fusion(bf16[32,6,10,256]{3,0,2,1:T(8,128)(2,1)S(1)} %copy.228, ...), kind=kLoop, calls=%fused_computation.193 | loop fusion | flops 9437184 | bytes 5705472 | tf_op jit(solution)/shard_map/stack | solution.py:31
  59.3 5.1 %fusion.92 = (bf16[1,32,4,8,256]{4,1,3,2,0:T(8,128)(2,1)S(1)}, bf16[1,32,4,8,256]{4,1,3,2,0:T(8,128)(2,1)S(1)}, bf16[1,32,4,8,256]{4,1,3,2,0:T(8,128)(2,1)S(1)},...) fusion(bf16[32,6,10,1]{3,0,2,1:T(8,128)(2,1)} %copy.232, ...), kind=kLoop, calls=%fused_computation.189 | loop fusion | flops 9437184 | bytes 5705472 | tf_op jit(solution)/shard_map/stack | solution.py:31
  66.7 2.2 copy_dynamic-update-slice_fusion.46
  81.0 1.6 copy_dynamic-update-slice_fusion.26
  84.7 8.4 %reshape.195 = bf16[288,8192]{1,0:T(8,128)(2,1)} reshape(bf16[9,32,4,8,256]{4,3,2,1,0:T(8,128)(2,1)} %copy_dynamic-update-slice_fusion.24) | data formatting | bytes 9437184 | tf_op jit(solution)/shard_map/reshape | solution.py:39
  93.1 2.1 copy_dynamic-update-slice_fusion.33
  96.3 8.5 %reshape.193 = bf16[288,8192]{1,0:T(8,128)(2,1)} reshape(bf16[9,32,4,8,256]{4,3,2,1,0:T(8,128)(2,1)} %copy_dynamic-update-slice_fusion.32) | data formatting | bytes 9437184 | tf_op jit(solution)/shard_map/reshape | solution.py:39
  109.2 8.3 %reshape.191 = bf16[288,8192]{1,0:T(8,128)(2,1)} reshape(bf16[9,32,4,8,256]{4,3,2,1,0:T(8,128)(2,1)} %copy_dynamic-update-slice_fusion.40) | data formatting | bytes 9437184 | tf_op jit(solution)/shard_map/reshape | solution.py:39
  117.5 3.5 %fusion.114 = f32[8192,32]{0,1:T(8,128)S(1)} fusion(bf16[32,288]{1,0:T(8,128)(2,1)S(1)} %reshape.192, bf16[288,8192]{1,0:T(8,128)(2,1)} %reshape.191), kind=kOutput, calls=%fused_computation.291 | convolution fusion | flops 150994944 | bytes 5785600 | tf_op jit(solution)/shard_map/dot_general | solution.py:41
  120.9 3.4 %convolution_add_fusion.3 = f32[8192,32]{0,1:T(8,128)S(1)} fusion(f32[8192,32]{0,1:T(8,128)S(1)} %fusion.114, bf16[32,288]{1,0:T(8,128)(2,1)S(1)} %reshape.194, bf16[288,8192]{1,0:T(8,128)(2,1)} %reshape.193), kind=kOutput, calls=%fused_computation.5 | convolution fusion | flops 151257088 | bytes 6834176 | tf_op jit(solution)/shard_map/dot_general | solution.py:41
  125.6 4.3 %collective-permute-start.6 = (bf16[32,1,8,256]{3,2,1,0:T(8,128)(2,1)S(1)}, bf16[32,1,8,256]{3,2,1,0:T(8,128)(2,1)S(1)}, u32[]{:S(2)}, u32[]{:S(2)}) collective-permute-start(bf16[32,1,8,256]{3,2,1,0:T(8,128)(2,1)S(1)} %get-tuple-element.69), channel_id=1, source_target_pairs={{0,4},{4,8},{8,12},{1,5},{5,9},{9,13},{2,6},{6,10},{10,14},{3,7},{... | collective-permute-start | bytes 393224 | tf_op jit(solution)/shard_map/ppermute | solution.py:16
  132.2 1.3 collective-permute-start.7
  133.6 6.7 %collective-permute-done.7 = bf16[32,1,8,256]{3,2,1,0:T(8,128)(2,1)S(1)} collective-permute-done((bf16[32,1,8,256]{3,2,1,0:T(8,128)(2,1)S(1)}, bf16[32,1,8,256]{3,2,1,0:T(8,128)(2,1)S(1)}, u32[]{:S(2)}, u32[]{:S(2)}) %collective-permute-start.7) | collective-permute-done | bytes 131104 | tf_op jit(solution)/shard_map/ppermute | solution.py:17
  140.4 3.5 %copy.262 = bf16[32,6,8,256]{0,1,3,2:T(8,128)(2,1)} copy(bf16[32,6,8,256]{3,2,1,0:T(8,128)(2,1)S(1)} %constant_dynamic-update-slice_fusion.3) | data formatting | bytes 1572864 | tf_op jit(solution)/shard_map/concatenate | solution.py:18
  143.9 1.4 fusion.110
  145.3 1.6 collective-permute-start.8
  146.9 1.3 collective-permute-start.9
  149.0 9.2 %collective-permute-done.8 = bf16[32,6,1,256]{0,1,3,2:T(8,128)(2,1)S(1)} collective-permute-done((bf16[32,6,1,256]{0,1,3,2:T(8,128)(2,1)S(1)}, bf16[32,6,1,256]{0,1,3,2:T(8,128)(2,1)S(1)}, u32[]{:S(2)}, u32[]{:S(2)}) %collective-permute-start.8) | collective-permute-done | bytes 98336 | tf_op jit(solution)/shard_map/ppermute | solution.py:16
  158.2 4.1 %collective-permute-done.9 = bf16[32,6,1,256]{0,1,3,2:T(8,128)(2,1)S(1)} collective-permute-done((bf16[32,6,1,256]{0,1,3,2:T(8,128)(2,1)S(1)}, bf16[32,6,1,256]{0,1,3,2:T(8,128)(2,1)S(1)}, u32[]{:S(2)}, u32[]{:S(2)}) %collective-permute-start.9) | collective-permute-done | bytes 98336 | tf_op jit(solution)/shard_map/ppermute | solution.py:17
  162.3 4.0 %pad_maximum_fusion.1 = bf16[32,6,10,256]{0,1,3,2:T(8,128)(2,1)S(1)} fusion(bf16[32,6,1,256]{0,1,3,2:T(8,128)(2,1)S(1)} %collective-permute-done.9, bf16[32,6,8,256]{0,1,3,2:T(8,128)(2,1)} %copy.262, bf16[32,6,1,256]{0,1,3,2:T(8,128)(2,1)S(1)} %collective-permute-done.8), kind=kLoop, calls=%fused_computation.8 | loop fusion | flops 983040 | bytes 1966080 | tf_op jit(solution)/shard_map/concatenate | solution.py:18
  166.4 2.3 copy-done.1
  173.5 1.7 fusion.85
  175.2 4.7 %copy.266 = bf16[32,6,10,256]{3,0,2,1:T(8,128)(2,1)S(1)} copy(bf16[32,6,10,256]{0,1,3,2:T(8,128)(2,1)} %copy-done.1) | data formatting | bytes 1966080 | tf_op jit(solution)/shard_map/concatenate | solution.py:18
  180.5 3.7 %fusion.86 = (bf16[1,32,4,8,256]{4,1,3,2,0:T(8,128)(2,1)}, bf16[1,32,4,8,256]{4,1,3,2,0:T(8,128)(2,1)S(1)}, bf16[1,32,4,8,256]{4,1,3,2,0:T(8,128)(2,1)}, bf16[1,...) fusion(bf16[32,6,10,256]{3,0,2,1:T(8,128)(2,1)S(1)} %copy.266, ...), kind=kLoop, calls=%fused_computation.179 | loop fusion | flops 9437184 | bytes 5705472 | tf_op jit(solution)/shard_map/stack | solution.py:31
  186.5 5.4 %fusion.84 = (bf16[1,32,4,8,256]{4,1,3,2,0:T(8,128)(2,1)S(1)}, bf16[1,32,4,8,256]{4,1,3,2,0:T(8,128)(2,1)S(1)}, bf16[1,32,4,8,256]{4,1,3,2,0:T(8,128)(2,1)}, bf1...) fusion(bf16[32,6,10,1]{3,0,2,1:T(8,128)(2,1)} %copy.270, ...), kind=kLoop, calls=%fused_computation.175 | loop fusion | flops 9437184 | bytes 5705472 | tf_op jit(solution)/shard_map/stack | solution.py:31
  193.0 2.2 copy_dynamic-update-slice_fusion.22
  206.1 8.3 %reshape.201 = bf16[288,8192]{1,0:T(8,128)(2,1)} reshape(bf16[9,32,4,8,256]{4,3,2,1,0:T(8,128)(2,1)} %copy_dynamic-update-slice_fusion) | data formatting | bytes 9437184 | tf_op jit(solution)/shard_map/reshape | solution.py:39
  214.4 2.3 copy_dynamic-update-slice_fusion.15
  216.7 2.1 copy_dynamic-update-slice_fusion.14
  218.8 2.1 copy_dynamic-update-slice_fusion.13
  221.0 2.1 copy_dynamic-update-slice_fusion.12
  228.3 8.6 %reshape.199 = bf16[288,8192]{1,0:T(8,128)(2,1)} reshape(bf16[9,32,4,8,256]{4,3,2,1,0:T(8,128)(2,1)} %copy_dynamic-update-slice_fusion.8) | data formatting | bytes 9437184 | tf_op jit(solution)/shard_map/reshape | solution.py:39
  241.3 8.3 %reshape.197 = bf16[288,8192]{1,0:T(8,128)(2,1)} reshape(bf16[9,32,4,8,256]{4,3,2,1,0:T(8,128)(2,1)} %copy_dynamic-update-slice_fusion.16) | data formatting | bytes 9437184 | tf_op jit(solution)/shard_map/reshape | solution.py:39
  249.6 3.5 %fusion.115 = f32[8192,32]{0,1:T(8,128)S(1)} fusion(bf16[32,288]{1,0:T(8,128)(2,1)S(1)} %copy-done.32, bf16[288,8192]{1,0:T(8,128)(2,1)} %reshape.197), kind=kOutput, calls=%fused_computation.292 | convolution fusion | flops 150994944 | bytes 5785600 | tf_op jit(solution)/shard_map/dot_general | solution.py:41
  253.1 3.4 %convolution_add_fusion.1 = f32[8192,32]{0,1:T(8,128)S(1)} fusion(f32[8192,32]{0,1:T(8,128)S(1)} %fusion.115, bf16[32,288]{1,0:T(8,128)(2,1)S(1)} %copy-done.33, bf16[288,8192]{1,0:T(8,128)(2,1)} %reshape.199), kind=kOutput, calls=%fused_computation.2 | convolution fusion | flops 151257088 | bytes 6834176 | tf_op jit(solution)/shard_map/dot_general | solution.py:41
  260.2 13.4 %all_gather.3 = bf16[4,32,256]{2,1,0:T(8,128)(2,1)S(1)} all-gather(bf16[1,32,256]{2,1,0:T(8,128)(2,1)S(1)} %divide_convert_fusion), channel_id=1, replica_groups=mesh['group'=2,'gz'=4,'gy'=2,'gx'=2] {'gz'}, dimensions={0}, use_global_device_ids=true | all-gather | bytes 81920 | tf_op jit(solution)/shard_map/all_gather | solution.py:68
  (195 shorter events, 73.7 us)
Async XLA Ops:
  1.6 9.6 %collective-permute-start = (bf16[32,1,8,256]{3,2,1,0:T(8,128)(2,1)S(1)}, bf16[32,1,8,256]{3,2,1,0:T(8,128)(2,1)S(1)}, u32[]{:S(2)}, u32[]{:S(2)}) collective-permute-start(bf16[32,1,8,256]{3,2,1,0:T(8,128)(2,1)S(1)} %get-tuple-element.74), channel_id=1, source_target_pairs={{0,4},{4,8},{8,12},{1,5},{5,9},{9,13},{2,6},{6,10},{10,14},{3,7},{... | collective-permute-start | bytes 393224 | tf_op jit(solution)/shard_map/ppermute | solution.py:16
  6.6 17.5 %copy-start.37 = (s32[1,1,1,256]{3,2,1,0:T(1,128)S(1)}, s32[1,1,1,256]{3,2,1,0:T(1,128)}, u32[]{:S(2)}) copy-start(s32[1,1,1,256]{3,2,1,0:T(1,128)} %param.9) | copy-start | bytes 3076
  6.6 6.9 %collective-permute-start.1 = (bf16[32,1,8,256]{3,2,1,0:T(8,128)(2,1)S(1)}, bf16[32,1,8,256]{3,2,1,0:T(8,128)(2,1)S(1)}, u32[]{:S(2)}, u32[]{:S(2)}) collective-permute-start(bf16[32,1,8,256]{3,2,1,0:T(8,128)(2,1)S(1)} %get-tuple-element.73), channel_id=1, source_target_pairs={{4,0},{8,4},{12,8},{5,1},{9,5},{13,9},{6,2},{10,6},{14,10},{7,3},{... | collective-permute-start | bytes 393224 | tf_op jit(solution)/shard_map/ppermute | solution.py:17
  19.4 13.5 %collective-permute-start.2 = (bf16[32,6,1,256]{0,1,3,2:T(8,128)(2,1)}, bf16[32,6,1,256]{0,1,3,2:T(8,128)(2,1)S(1)}, u32[]{:S(2)}, u32[]{:S(2)}) collective-permute-start(bf16[32,6,1,256]{0,1,3,2:T(8,128)(2,1)} %get-tuple-element.10), channel_id=1, source_target_pairs={{0,2},{1,3},{4,6},{5,7},{8,10},{9,11},{12,14},{13,15},{16,18},{17,... | collective-permute-start | bytes 294920 | tf_op jit(solution)/shard_map/ppermute | solution.py:16
  22.8 14.1 %collective-permute-start.3 = (bf16[32,6,1,256]{0,1,3,2:T(8,128)(2,1)}, bf16[32,6,1,256]{0,1,3,2:T(8,128)(2,1)S(1)}, u32[]{:S(2)}, u32[]{:S(2)}) collective-permute-start(bf16[32,6,1,256]{0,1,3,2:T(8,128)(2,1)} %get-tuple-element.11), channel_id=1, source_target_pairs={{2,0},{3,1},{6,4},{7,5},{10,8},{11,9},{14,12},{15,13},{18,16},{19,... | collective-permute-start | bytes 294920 | tf_op jit(solution)/shard_map/ppermute | solution.py:17
  43.0 9.9 %collective-permute-start.4 = (bf16[32,6,10,1]{0,1,3,2:T(8,128)(2,1)S(1)}, bf16[32,6,10,1]{0,1,3,2:T(8,128)(2,1)S(1)}, u32[]{:S(2)}, u32[]{:S(2)}) collective-permute-start(bf16[32,6,10,1]{0,1,3,2:T(8,128)(2,1)S(1)} %get-tuple-element.7), channel_id=1, source_target_pairs={{0,1},{2,3},{4,5},{6,7},{8,9},{10,11},{12,13},{14,15},{16,17},{18,... | collective-permute-start | bytes 11528 | tf_op jit(solution)/shard_map/ppermute | solution.py:16
  44.3 13.8 %collective-permute-start.5 = (bf16[32,6,10,1]{0,1,3,2:T(8,128)(2,1)S(1)}, bf16[32,6,10,1]{0,1,3,2:T(8,128)(2,1)S(1)}, u32[]{:S(2)}, u32[]{:S(2)}) collective-permute-start(bf16[32,6,10,1]{0,1,3,2:T(8,128)(2,1)S(1)} %get-tuple-element.6), channel_id=1, source_target_pairs={{1,0},{3,2},{5,4},{7,6},{9,8},{11,10},{13,12},{15,14},{17,16},{19,... | collective-permute-start | bytes 11528 | tf_op jit(solution)/shard_map/ppermute | solution.py:17
  59.3 10.6 %copy-start.12 = (bf16[1,32,4,8,256]{4,1,3,2,0:T(8,128)(2,1)S(1)}, bf16[1,32,4,8,256]{4,1,3,2,0:T(8,128)(2,1)}, u32[]{:S(2)}) copy-start(bf16[1,32,4,8,256]{4,1,3,2,0:T(8,128)(2,1)} %get-tuple-element.41) | copy-start | bytes 1572868
  59.3 11.7 %copy-start.26 = (bf16[1,32,4,8,256]{4,1,3,2,0:T(8,128)(2,1)S(1)}, bf16[1,32,4,8,256]{4,1,3,2,0:T(8,128)(2,1)}, u32[]{:S(2)}) copy-start(bf16[1,32,4,8,256]{4,1,3,2,0:T(8,128)(2,1)} %get-tuple-element.63) | copy-start | bytes 1572868
  64.4 8.7 %copy-start.10 = (bf16[1,32,4,8,256]{4,1,3,2,0:T(8,128)(2,1)S(1)}, bf16[1,32,4,8,256]{4,1,3,2,0:T(8,128)(2,1)}, u32[]{:S(2)}) copy-start(bf16[1,32,4,8,256]{4,1,3,2,0:T(8,128)(2,1)} %get-tuple-element.44) | copy-start | bytes 1572868
  64.4 9.8 %copy-start.25 = (bf16[1,32,4,8,256]{4,1,3,2,0:T(8,128)(2,1)S(1)}, bf16[1,32,4,8,256]{4,1,3,2,0:T(8,128)(2,1)}, u32[]{:S(2)}) copy-start(bf16[1,32,4,8,256]{4,1,3,2,0:T(8,128)(2,1)} %get-tuple-element.65) | copy-start | bytes 1572868
  65.6 10.9 %copy-start.9 = (bf16[1,32,4,8,256]{4,1,3,2,0:T(8,128)(2,1)S(1)}, bf16[1,32,4,8,256]{4,1,3,2,0:T(8,128)(2,1)}, u32[]{:S(2)}) copy-start(bf16[1,32,4,8,256]{4,1,3,2,0:T(8,128)(2,1)} %get-tuple-element.47) | copy-start | bytes 1572868
  66.6 10.9 %copy-start.2 = (bf16[32,4,8,256]{3,2,1,0:T(8,128)(2,1)S(1)}, bf16[32,4,8,256]{3,2,1,0:T(8,128)(2,1)}, u32[]{:S(2)}) copy-start(bf16[32,4,8,256]{3,2,1,0:T(8,128)(2,1)} %param.6) | copy-start | bytes 1572868
  72.1 8.9 %copy-start.17 = (bf16[1,32,4,8,256]{4,1,3,2,0:T(8,128)(2,1)S(1)}, bf16[1,32,4,8,256]{4,1,3,2,0:T(8,128)(2,1)}, u32[]{:S(2)}) copy-start(bf16[1,32,4,8,256]{4,1,3,2,0:T(8,128)(2,1)} %get-tuple-element.39) | copy-start | bytes 1572868
  72.1 8.9 %copy-start.18 = (bf16[1,32,4,8,256]{4,1,3,2,0:T(8,128)(2,1)S(1)}, bf16[1,32,4,8,256]{4,1,3,2,0:T(8,128)(2,1)}, u32[]{:S(2)}) copy-start(bf16[1,32,4,8,256]{4,1,3,2,0:T(8,128)(2,1)} %get-tuple-element.45) | copy-start | bytes 1572868
  74.3 8.3 %copy-start.23 = (bf16[1,32,4,8,256]{4,1,3,2,0:T(8,128)(2,1)S(1)}, bf16[1,32,4,8,256]{4,1,3,2,0:T(8,128)(2,1)}, u32[]{:S(2)}) copy-start(bf16[1,32,4,8,256]{4,1,3,2,0:T(8,128)(2,1)} %get-tuple-element.54) | copy-start | bytes 1572868
  84.7 10.5 %copy-start.5 = (bf16[1,32,4,8,256]{4,1,3,2,0:T(8,128)(2,1)S(1)}, bf16[1,32,4,8,256]{4,1,3,2,0:T(8,128)(2,1)}, u32[]{:S(2)}) copy-start(bf16[1,32,4,8,256]{4,1,3,2,0:T(8,128)(2,1)} %get-tuple-element.36) | copy-start | bytes 1572868
  96.3 10.7 %copy-start.20 = (bf16[1,32,4,8,256]{4,1,3,2,0:T(8,128)(2,1)S(1)}, bf16[1,32,4,8,256]{4,1,3,2,0:T(8,128)(2,1)}, u32[]{:S(2)}) copy-start(bf16[1,32,4,8,256]{4,1,3,2,0:T(8,128)(2,1)} %get-tuple-element.55) | copy-start | bytes 1572868
  117.5 6.9 %slice-start.2 = ((s8[4718592]{0:T(1024)(128)(4,1)}), s8[4194304]{0:T(1024)(128)(4,1)S(1)}, s32[]{:S(2)}) async-start(s8[4718592]{0:T(1024)(128)(4,1)} %bitcast.207), calls=%async_computation.2 | async-start | bytes 8388608
  124.4 5.5 %copy-start.34 = (s32[4,1,1,256]{3,2,1,0:T(1,128)S(1)}, s32[4,1,1,256]{3,2,1,0:T(1,128)}, u32[]{:S(2)}) copy-start(s32[4,1,1,256]{3,2,1,0:T(1,128)} %param.10) | copy-start | bytes 12292
  124.4 6.1 %copy-start.31 = (bf16[32,3,3,32]{3,0,2,1:T(8,128)(2,1)S(1)}, bf16[32,3,3,32]{3,0,2,1:T(8,128)(2,1)}, u32[]{:S(2)}) copy-start(bf16[32,3,3,32]{3,0,2,1:T(8,128)(2,1)} %get-tuple-element.76) | copy-start | bytes 55300
  124.4 6.8 %copy-start.30 = (bf16[32,3,3,32]{3,0,2,1:T(8,128)(2,1)S(1)}, bf16[32,3,3,32]{3,0,2,1:T(8,128)(2,1)}, u32[]{:S(2)}) copy-start(bf16[32,3,3,32]{3,0,2,1:T(8,128)(2,1)} %get-tuple-element.77) | copy-start | bytes 55300
  124.4 7.7 %copy-start.36 = (s32[4,4]{1,0:T(4,128)S(1)}, s32[4,4]{1,0:T(4,128)}, u32[]{:S(2)}) copy-start(s32[4,4]{1,0:T(4,128)} %param.11) | copy-start | bytes 196
  125.6 8.0 %collective-permute-start.6 = (bf16[32,1,8,256]{3,2,1,0:T(8,128)(2,1)S(1)}, bf16[32,1,8,256]{3,2,1,0:T(8,128)(2,1)S(1)}, u32[]{:S(2)}, u32[]{:S(2)}) collective-permute-start(bf16[32,1,8,256]{3,2,1,0:T(8,128)(2,1)S(1)} %get-tuple-element.69), channel_id=1, source_target_pairs={{0,4},{4,8},{8,12},{1,5},{5,9},{9,13},{2,6},{6,10},{10,14},{3,7},{... | collective-permute-start | bytes 393224 | tf_op jit(solution)/shard_map/ppermute | solution.py:16
  132.2 8.1 %collective-permute-start.7 = (bf16[32,1,8,256]{3,2,1,0:T(8,128)(2,1)S(1)}, bf16[32,1,8,256]{3,2,1,0:T(8,128)(2,1)S(1)}, u32[]{:S(2)}, u32[]{:S(2)}) collective-permute-start(bf16[32,1,8,256]{3,2,1,0:T(8,128)(2,1)S(1)} %get-tuple-element.68), channel_id=1, source_target_pairs={{4,0},{8,4},{12,8},{5,1},{9,5},{13,9},{6,2},{10,6},{14,10},{7,3},{... | collective-permute-start | bytes 393224 | tf_op jit(solution)/shard_map/ppermute | solution.py:17
  140.3 26.0 %copy-start.28 = (bf16[32,1,8,256]{3,2,1,0:T(8,128)(2,1)}, bf16[32,1,8,256]{3,2,1,0:T(8,128)(2,1)S(1)}, u32[]{:S(2)}) copy-start(bf16[32,1,8,256]{3,2,1,0:T(8,128)(2,1)S(1)} %collective-permute-done.7) | copy-start | bytes 393220
  145.3 12.9 %collective-permute-start.8 = (bf16[32,6,1,256]{0,1,3,2:T(8,128)(2,1)S(1)}, bf16[32,6,1,256]{0,1,3,2:T(8,128)(2,1)S(1)}, u32[]{:S(2)}, u32[]{:S(2)}) collective-permute-start(bf16[32,6,1,256]{0,1,3,2:T(8,128)(2,1)S(1)} %get-tuple-element.8), channel_id=1, source_target_pairs={{0,2},{1,3},{4,6},{5,7},{8,10},{9,11},{12,14},{13,15},{16,18},{17,... | collective-permute-start | bytes 294920 | tf_op jit(solution)/shard_map/ppermute | solution.py:16
  146.9 15.4 %collective-permute-start.9 = (bf16[32,6,1,256]{0,1,3,2:T(8,128)(2,1)S(1)}, bf16[32,6,1,256]{0,1,3,2:T(8,128)(2,1)S(1)}, u32[]{:S(2)}, u32[]{:S(2)}) collective-permute-start(bf16[32,6,1,256]{0,1,3,2:T(8,128)(2,1)S(1)} %get-tuple-element.9), channel_id=1, source_target_pairs={{2,0},{3,1},{6,4},{7,5},{10,8},{11,9},{14,12},{15,13},{18,16},{19,... | collective-permute-start | bytes 294920 | tf_op jit(solution)/shard_map/ppermute | solution.py:17
  169.3 10.6 %collective-permute-start.10 = (bf16[32,6,10,1]{0,1,3,2:T(8,128)(2,1)}, bf16[32,6,10,1]{0,1,3,2:T(8,128)(2,1)S(1)}, u32[]{:S(2)}, u32[]{:S(2)}) collective-permute-start(bf16[32,6,10,1]{0,1,3,2:T(8,128)(2,1)} %get-tuple-element.5), channel_id=1, source_target_pairs={{0,1},{2,3},{4,5},{6,7},{8,9},{10,11},{12,13},{14,15},{16,17},{18,... | collective-permute-start | bytes 11528 | tf_op jit(solution)/shard_map/ppermute | solution.py:16
  170.6 14.6 %collective-permute-start.11 = (bf16[32,6,10,1]{0,1,3,2:T(8,128)(2,1)}, bf16[32,6,10,1]{0,1,3,2:T(8,128)(2,1)S(1)}, u32[]{:S(2)}, u32[]{:S(2)}) collective-permute-start(bf16[32,6,10,1]{0,1,3,2:T(8,128)(2,1)} %get-tuple-element.4), channel_id=1, source_target_pairs={{1,0},{3,2},{5,4},{7,6},{9,8},{11,10},{13,12},{15,14},{17,16},{19,... | collective-permute-start | bytes 11528 | tf_op jit(solution)/shard_map/ppermute | solution.py:17
  186.5 5.4 %copy-start.16 = (bf16[1,32,4,8,256]{4,1,3,2,0:T(8,128)(2,1)S(1)}, bf16[1,32,4,8,256]{4,1,3,2,0:T(8,128)(2,1)}, u32[]{:S(2)}) copy-start(bf16[1,32,4,8,256]{4,1,3,2,0:T(8,128)(2,1)} %get-tuple-element.28) | copy-start | bytes 1572868
  186.5 9.8 %copy-start.13 = (bf16[1,32,4,8,256]{4,1,3,2,0:T(8,128)(2,1)S(1)}, bf16[1,32,4,8,256]{4,1,3,2,0:T(8,128)(2,1)}, u32[]{:S(2)}) copy-start(bf16[1,32,4,8,256]{4,1,3,2,0:T(8,128)(2,1)} %get-tuple-element.23) | copy-start | bytes 1572868
  186.5 10.9 %copy-start.27 = (bf16[1,32,4,8,256]{4,1,3,2,0:T(8,128)(2,1)S(1)}, bf16[1,32,4,8,256]{4,1,3,2,0:T(8,128)(2,1)}, u32[]{:S(2)}) copy-start(bf16[1,32,4,8,256]{4,1,3,2,0:T(8,128)(2,1)} %get-tuple-element.62) | copy-start | bytes 1572868
  186.5 13.1 %copy-start.11 = (bf16[1,32,4,8,256]{4,1,3,2,0:T(8,128)(2,1)S(1)}, bf16[1,32,4,8,256]{4,1,3,2,0:T(8,128)(2,1)}, u32[]{:S(2)}) copy-start(bf16[1,32,4,8,256]{4,1,3,2,0:T(8,128)(2,1)} %get-tuple-element.29) | copy-start | bytes 1572868
  191.9 8.7 %copy-start.29 = (bf16[32,1,8,256]{3,2,1,0:T(8,128)(2,1)S(1)}, bf16[32,1,8,256]{3,2,1,0:T(8,128)(2,1)}, u32[]{:S(2)}) copy-start(bf16[32,1,8,256]{3,2,1,0:T(8,128)(2,1)} %copy-done.28) | copy-start | bytes 393220
  193.0 9.9 %copy-start.8 = (bf16[1,32,4,8,256]{4,1,3,2,0:T(8,128)(2,1)S(1)}, bf16[1,32,4,8,256]{4,1,3,2,0:T(8,128)(2,1)}, u32[]{:S(2)}) copy-start(bf16[1,32,4,8,256]{4,1,3,2,0:T(8,128)(2,1)} %get-tuple-element.21) | copy-start | bytes 1572868
  195.2 8.8 %copy-start.24 = (bf16[1,32,4,8,256]{4,1,3,2,0:T(8,128)(2,1)S(1)}, bf16[1,32,4,8,256]{4,1,3,2,0:T(8,128)(2,1)}, u32[]{:S(2)}) copy-start(bf16[1,32,4,8,256]{4,1,3,2,0:T(8,128)(2,1)} %get-tuple-element.48) | copy-start | bytes 1572868
  214.4 9.5 %copy-start.7 = (bf16[1,32,4,8,256]{4,1,3,2,0:T(8,128)(2,1)S(1)}, bf16[1,32,4,8,256]{4,1,3,2,0:T(8,128)(2,1)}, u32[]{:S(2)}) copy-start(bf16[1,32,4,8,256]{4,1,3,2,0:T(8,128)(2,1)} %get-tuple-element.17) | copy-start | bytes 1572868
  214.4 10.6 %copy-start.3 = (bf16[1,32,4,8,256]{4,1,3,2,0:T(8,128)(2,1)S(1)}, bf16[1,32,4,8,256]{4,1,3,2,0:T(8,128)(2,1)}, u32[]{:S(2)}) copy-start(bf16[1,32,4,8,256]{4,1,3,2,0:T(8,128)(2,1)} %get-tuple-element.27) | copy-start | bytes 1572868
  214.4 11.7 %copy-start.22 = (bf16[1,32,4,8,256]{4,1,3,2,0:T(8,128)(2,1)S(1)}, bf16[1,32,4,8,256]{4,1,3,2,0:T(8,128)(2,1)}, u32[]{:S(2)}) copy-start(bf16[1,32,4,8,256]{4,1,3,2,0:T(8,128)(2,1)} %get-tuple-element.50) | copy-start | bytes 1572868
  214.4 12.8 %copy-start.6 = (bf16[1,32,4,8,256]{4,1,3,2,0:T(8,128)(2,1)S(1)}, bf16[1,32,4,8,256]{4,1,3,2,0:T(8,128)(2,1)}, u32[]{:S(2)}) copy-start(bf16[1,32,4,8,256]{4,1,3,2,0:T(8,128)(2,1)} %get-tuple-element.18) | copy-start | bytes 1572868
  228.3 8.6 %copy-start.4 = (bf16[1,32,4,8,256]{4,1,3,2,0:T(8,128)(2,1)S(1)}, bf16[1,32,4,8,256]{4,1,3,2,0:T(8,128)(2,1)}, u32[]{:S(2)}) copy-start(bf16[1,32,4,8,256]{4,1,3,2,0:T(8,128)(2,1)} %get-tuple-element.14) | copy-start | bytes 1572868
  228.3 10.8 %copy-start.21 = (bf16[1,32,4,8,256]{4,1,3,2,0:T(8,128)(2,1)S(1)}, bf16[1,32,4,8,256]{4,1,3,2,0:T(8,128)(2,1)}, u32[]{:S(2)}) copy-start(bf16[1,32,4,8,256]{4,1,3,2,0:T(8,128)(2,1)} %get-tuple-element.49) | copy-start | bytes 1572868
  241.3 8.3 %copy-start.32 = (bf16[32,288]{1,0:T(8,128)(2,1)S(1)}, bf16[32,288]{1,0:T(8,128)(2,1)}, u32[]{:S(2)}) copy-start(bf16[32,288]{1,0:T(8,128)(2,1)} %reshape.198) | copy-start | bytes 55300
  249.6 6.9 %slice-start = ((s8[4718592]{0:T(1024)(128)(4,1)}), s8[4194304]{0:T(1024)(128)(4,1)S(1)}, s32[]{:S(2)}) async-start(s8[4718592]{0:T(1024)(128)(4,1)} %bitcast.205), calls=%async_computation | async-start | bytes 8388608
  257.5 16.0 %copy-start.38 = (s32[1,1,1,256]{3,2,1,0:T(1,128)S(1)}, s32[1,1,1,256]{3,2,1,0:T(1,128)}, u32[]{:S(2)}) copy-start(s32[1,1,1,256]{3,2,1,0:T(1,128)} %constant_dynamic-slice_fusion) | copy-start | bytes 3076
  257.5 16.0 %copy-start.39 = (f32[4]{0:T(128)S(1)}, f32[4]{0:T(128)}, u32[]{:S(2)}) copy-start(f32[4]{0:T(128)} %dynamic-slice_bitcast_fusion) | copy-start | bytes 52
  258.1 16.6 %copy-start.19 = (bf16[32,4,8,256]{3,2,1,0:T(8,128)(2,1)}, bf16[32,4,8,256]{3,2,1,0:T(8,128)(2,1)S(1)}, u32[]{:S(2)}) copy-start(bf16[32,4,8,256]{3,2,1,0:T(8,128)(2,1)S(1)} %add_convert_fusion) | copy-start | bytes 1572868
  (8 other events, 26.8 us)
where the time goes:
time: 280 us; the launch traced here: 275 us
  local copies, waits for them, and re-layouts  153 us (55%)
  other arithmetic  33.5 us (12%)
  waiting for transfers between devices  32.7 us (12%)
  starting transfers between devices  25 us (9%)
  matrix products  16.3 us (6%)
  blocking collectives  13.4 us (5%)
    unnamed x137, local copies, waits for them, and re-layouts  59.9 us
    reshape x6, local copies, waits for them, and re-layouts, conv_valid(): patches = stacked.reshape(9 * channels, out_z * out_y * out_x)  50.3 us
    another operation x6, other arithmetic, conv_valid(): jnp.stack([plane[:, :, offset_y:offset_y + out_y, column_shift:column_shi...  21.2 us
    concatenate x8, local copies, waits for them, and re-layouts, extended(): shard = jnp.concatenate([before, shard, after], axis=dim)  16.9 us
    ppermute x6, starting transfers between devices, extended(): before = lax.ppermute(last, axis, up)  16.8 us
    ppermute x6, waiting for transfers between devices, extended(): before = lax.ppermute(last, axis, up)  16.6 us
    ppermute x6, waiting for transfers between devices, extended(): after = lax.ppermute(leading, axis, down)  16 us
    dot_general x6, matrix products, conv_valid(): jnp.dot(kernel, patches, preferred_element_type=jnp.float32)  15.8 us
  transfers between devices with their start and end apart: 12, of which 7 were waited for; matrix products, arithmetic and copies ran while one was open for 12% of the time, Pallas kernels for 0%

commit v1 on v0

v1 whole, which is shorter than its diff:
```python
import functools

import jax
import jax.numpy as jnp
from jax import lax
from jax.experimental import pallas as pl
from jax.experimental.pallas import tpu as pltpu
from jax.sharding import PartitionSpec as P

BF = jnp.bfloat16
F32 = jnp.float32
MESH = pl.DeviceIdType.MESH
DIRS = ((1, 0), (-1, 0), (0, 1), (0, -1), (1, 1), (1, -1), (-1, 1), (-1, -1))
NSEG = 64


def iota(shape, dim):
    return lax.broadcasted_iota(jnp.int32, shape, dim)


def mm(a, b):
    return jnp.dot(a, b, preferred_element_type=F32)


def mm_tn(a, b):
    return lax.dot_general(a, b, (((0,), (0,)), ((), ())), preferred_element_type=F32)


def one_hot(mask):
    return jnp.where(mask, 1.0, 0.0).astype(BF)


def kernel(n_gz, n_gy, vol, wt1, wt2, sidx, seg, bm, feat, loss,
           xa, xh, xac, xhc, edge, band, band_halo, emb_all, acc,
           send_sem, recv_sem, xs_sem, xr_sem, es_sem, er_sem):
    gz, gy, gx = lax.axis_index("gz"), lax.axis_index("gy"), lax.axis_index("gx")
    other = 1 - gx

    def inside(dz, dy):
        z, y = gz + dz, gy + dy
        return (z >= 0) & (z < n_gz) & (y >= 0) & (y < n_gy)

    def dev(z, y, x):
        return {"gz": z, "gy": y, "gx": x}

    barrier = pltpu.get_barrier_semaphore()
    count = jnp.int32(n_gz)
    pl.semaphore_signal(barrier, inc=1, device_id=dev(gz, gy, other), device_id_type=MESH)
    for off in range(1, n_gz):
        pl.semaphore_signal(barrier, inc=1, device_id=dev(lax.rem(gz + off, n_gz), gy, gx), device_id_type=MESH)
    for dz, dy in DIRS:
        if dy != 0:
            there = inside(dz, dy)
            count = count + there.astype(jnp.int32)

            @pl.when(there)
            def _():
                pl.semaphore_signal(barrier, inc=1, device_id=dev(gz + dz, gy + dy, gx), device_id_type=MESH)

    def halo_copy(r, d):
        dz, dy = DIRS[d]
        side = slice(0, 32) if dy == 1 else slice(32, 64)
        if dy == 0:
            src = xa.at[r, 4 if dz == 1 else 1]
            dst = xa.at[r, 0 if dz == 1 else 5]
        elif dz == 0:
            src, dst = edge.at[r, :, side, :], xh.at[r, 1:5, side, :]
        else:
            src = edge.at[r, 3 if dz == 1 else 0, side, :]
            dst = xh.at[r, 0 if dz == 1 else 5, side, :]
        return pltpu.make_async_remote_copy(
            src_ref=src, dst_ref=dst, send_sem=send_sem.at[r, d], recv_sem=recv_sem.at[r, d],
            device_id=dev(gz + dz, gy + dy, gx), device_id_type=MESH)

    near = pl.ds(pl.multiple_of(other * 128, 128), 128)

    def x_copy(r, j):
        if j == 3:
            src, dst = xh.at[r, :, :, near], xhc.at[r]
        else:
            planes = (slice(1, 5), slice(0, 1), slice(5, 6))[j]
            src, dst = xa.at[r, planes, :, near], xac.at[r, planes]
        return pltpu.make_async_remote_copy(
            src_ref=src, dst_ref=dst, send_sem=xs_sem.at[r, j], recv_sem=xr_sem.at[r, j],
            device_id=dev(gz, gy, other), device_id_type=MESH)

    def start_round(r):
        for d, (dz, dy) in enumerate(DIRS):
            @pl.when(inside(dz, dy))
            def _():
                halo_copy(r, d).start()
        x_copy(r, 0).start()

    def zero_missing(r):
        for dz, dy in DIRS:
            @pl.when(jnp.logical_not(inside(-dz, -dy)))
            def _():
                side = slice(0, 32) if dy == 1 else slice(32, 64)
                if dy == 0:
                    xa[r, 0 if dz == 1 else 5] = jnp.zeros((256, 256), BF)
                elif dz == 0:
                    xh[r, 1:5, side, :] = jnp.zeros((4, 32, 256), BF)
                else:
                    xh[r, 0 if dz == 1 else 5, side, :] = jnp.zeros((32, 256), BF)

    def finish_round(r):
        for d, (dz, dy) in enumerate(DIRS):
            @pl.when(inside(-dz, -dy))
            def _():
                halo_copy(r, d).wait_recv()
        for j in (1, 2, 3):
            x_copy(r, j).start()
        for j in range(4):
            x_copy(r, j).wait_recv()

    def drain_round(r):
        for d, (dz, dy) in enumerate(DIRS):
            @pl.when(inside(dz, dy))
            def _():
                halo_copy(r, d).wait_send()
        for j in range(4):
            x_copy(r, j).wait_send()

    er, ec = iota((64, 256), 0), iota((64, 256), 1)
    pick_edges = one_hot(ec == jnp.where(er < 32, er * 8 + 7, (er - 32) * 8))

    def keep(r, z, plane):
        xa[r, z + 1] = plane
        edge[r, z] = mm(pick_edges, plane).astype(BF)

    def build(r, wt):
        rows_out = one_hot((iota((256, 32), 0) >> 3) == iota((256, 32), 1))
        spread = one_hot(iota((96, 768), 0) == (iota((96, 768), 1) >> 3))
        hr, hc = iota((96, 192), 0), iota((96, 192), 1)
        home = hr == ((hc >> 6) * 32 + (hc & 31))
        low = one_hot(home & ((hc & 32) == 0))
        high = one_hot(home & ((hc & 32) != 0))
        tap = (iota((256, 768), 1) & 7) - (iota((256, 768), 0) & 7) + 1
        y = iota((256, 192), 0) & 7
        upper = (iota((256, 192), 1) & 32) != 0
        at_edge = y == jnp.where(upper, 7, 0)

        @pl.loop(0, 3)
        def _(c):
            total = jnp.zeros((256, 768), F32)
            for b in range(3):
                wide = mm(wt[c, b], spread).astype(BF)
                total = jnp.where(tap == b, mm(rows_out, wide), total)
            band[r, c] = total.astype(BF)
            ends = (mm(wt[c, 0], low) + mm(wt[c, 2], high)).astype(BF)
            band_halo[r, c] = jnp.where(at_edge, mm(rows_out, ends), 0.0).astype(BF)

    lane = iota((256, 256), 1)
    lane_half = iota((256, 128), 1)
    side_tap = 2 * other

    def conv(r, z):
        main = xa[r, pl.ds(z, 3)].reshape(768, 256)
        halo = xh[r, pl.ds(z, 3)].reshape(192, 256)
        p = [mm(band[r, c], main) + mm(band_halo[r, c], halo) for c in range(3)]
        q = mm(band[r, side_tap], xac[r, pl.ds(z, 3)].reshape(768, 128))
        q = q + mm(band_halo[r, side_tap], xhc[r, pl.ds(z, 3)].reshape(192, 128))
        out = p[1] + jnp.where(lane == 0, 0.0, pltpu.roll(p[0], 1, 1))
        out = out + jnp.where(lane == 255, 0.0, pltpu.roll(p[2], 255, 1))
        first = jnp.where(lane_half == gx - 1, pltpu.roll(q, 1, 1), 0.0)
        last = jnp.where(lane_half == 127 - 128 * gx, pltpu.roll(q, 127, 1), 0.0)
        return out + jnp.concatenate([first, last], axis=1)

    for z in range(4):
        keep(0, z, vol[:, z].astype(F32).reshape(256, 256).astype(BF))
    pl.semaphore_wait(barrier, count)
    start_round(0)
    zero_missing(0)
    zero_missing(1)
    build(0, wt1)
    finish_round(0)

    @pl.loop(0, 4)
    def _(z):
        keep(1, z, jnp.maximum(conv(0, z), 0.0).astype(BF))

    start_round(1)
    build(1, wt2)
    s = sidx[...]
    s_x, s_y, s_z = s & 255, (s >> 8) & 7, s >> 11
    select_x = one_hot(iota((256, 256), 0) == s_x)
    acc[...] = jnp.zeros((256, 256), F32)
    finish_round(1)

    @pl.loop(0, 4)
    def _(z):
        f = (conv(1, z) + xa[0, z + 1].astype(F32)).astype(BF)
        feat[:, z] = f.astype(F32).reshape(32, 8, 256).astype(BF)
        acc[...] = jnp.where(s_z == z, mm(f, select_x), acc[...])

    picked = jnp.where((iota((256, 256), 0) & 7) == s_y, acc[...], 0.0)
    picked = jnp.sum(picked.reshape(32, 8, 256), axis=1)
    norm = jnp.sqrt(jnp.sum(picked * picked, axis=0, keepdims=True) + 1.0)
    emb_all[0] = (picked / norm).astype(BF)

    def emb_copy(off):
        return pltpu.make_async_remote_copy(
            src_ref=emb_all.at[0], dst_ref=emb_all.at[off], send_sem=es_sem.at[off], recv_sem=er_sem.at[off],
            device_id=dev(lax.rem(gz + off, n_gz), gy, gx), device_id_type=MESH)

    for off in range(1, n_gz):
        emb_copy(off).start()
    drain_round(0)
    drain_round(1)
    own = emb_all[0]
    label = iota((NSEG, 256), 0)
    own_seg = one_hot(label == seg[pl.ds(gz, 1), :])
    total = jnp.zeros((1, 256), F32)
    positive = jnp.zeros((1, 256), F32)
    for off in range(n_gz):
        block = lax.rem(gz + n_gz - off, n_gz)
        if off:
            emb_copy(off).wait_recv()
        same = mm_tn(one_hot(label == seg[pl.ds(block, 1), :]), own_seg)
        e = jnp.exp(mm_tn(emb_all[off], own) * 4.0) * bm[gz, block].astype(F32)
        total = total + jnp.sum(e, axis=0, keepdims=True)
        positive = positive + jnp.sum(e * same, axis=0, keepdims=True)
    loss[...] = jnp.log(total) - jnp.log(positive)
    for off in range(1, n_gz):
        emb_copy(off).wait_send()


def by_tap(weight):
    return jnp.transpose(weight, (2, 1, 3, 0, 4)).reshape(3, 3, 32, 96)


def shards(n_gz, n_gy, volume, first_weight, second_weight, sample_index, segments, block_match):
    vmem = pl.BlockSpec(memory_space=pltpu.VMEM)
    dma = pltpu.SemaphoreType.DMA
    features, row_loss = pl.pallas_call(
        functools.partial(kernel, n_gz, n_gy),
        out_shape=(
            jax.ShapeDtypeStruct(volume.shape, BF),
            jax.ShapeDtypeStruct((1, 256), F32),
        ),
        in_specs=[vmem] * 5 + [pl.BlockSpec(memory_space=pltpu.SMEM)],
        out_specs=(vmem, vmem),
        scratch_shapes=[
            pltpu.VMEM((2, 6, 256, 256), BF),
            pltpu.VMEM((2, 6, 64, 256), BF),
            pltpu.VMEM((2, 6, 256, 128), BF),
            pltpu.VMEM((2, 6, 64, 128), BF),
            pltpu.VMEM((2, 4, 64, 256), BF),
            pltpu.VMEM((2, 3, 256, 768), BF),
            pltpu.VMEM((2, 3, 256, 192), BF),
            pltpu.VMEM((n_gz, 32, 256), BF),
            pltpu.VMEM((256, 256), F32),
            dma((2, 8)), dma((2, 8)), dma((2, 4)), dma((2, 4)), dma((n_gz,)), dma((n_gz,)),
        ],
        compiler_params=pltpu.CompilerParams(
            collective_id=0, has_side_effects=True, vmem_limit_bytes=40 << 20),
        name="voxel_contrast",
    )(
        volume, by_tap(first_weight), by_tap(second_weight), sample_index.reshape(1, 256),
        segments.reshape(segments.shape[0], 256), block_match,
    )
    return features, row_loss.reshape(1, 1, 1, 256)


def solution(mesh):
    in_specs = (
        P(None, ("group", "gz"), "gy", "gx"),
        P(),
        P(),
        P(("group", "gz"), "gy", "gx", None),
        P("group", "gy", "gx", None),
        P("group", None),
    )
    out_specs = (P(None, ("group", "gz"), "gy", "gx"), P(("group", "gz"), "gy", "gx", None))
    body = functools.partial(shards, mesh.shape["gz"], mesh.shape["gy"])
    return jax.shard_map(body, mesh=mesh, in_specs=in_specs, out_specs=out_specs, check_vma=False)
```

time: 280 us -> 36.1 us (0.13); the launches traced: 275 us -> 35.9 us
  local copies, waits for them, and re-layouts: 153 us -> 5.07 us
  other arithmetic: 33.5 us -> 0 us
  waiting for transfers between devices: 32.7 us -> 0 us
  Pallas kernels: 0 us -> 30.2 us
  starting transfers between devices: 25 us -> 0 us
  matrix products: 16.3 us -> 0 us
  blocking collectives: 13.4 us -> 0 us
    unnamed x137 -> x13, local copies, waits for them, and re-layouts: 59.9 us -> 3.5 us
    reshape x12 -> x2, local copies, waits for them, and re-layouts: 52.2 us -> 0.33 us  [by_tap(): return jnp.transpose(weight, (2, 1, 3, 0, 4)).reshape(3, 3, 32, 96)]
    ppermute x12 -> x0, waiting for transfers between devices: 32.7 us -> none  [the longest x6 16.6 us: extended(): before = lax.ppermute(last, axis, up)]
    pallas_call x0 -> x1, Pallas kernels: none -> 30.2 us  [shards(): pl.pallas_call(functools.partial(kernel, n_gz, n_gy), out_shape=(jax.Shap...]
    ppermute x12 -> x0, starting transfers between devices: 25 us -> none  [the longest x6 16.8 us: extended(): before = lax.ppermute(last, axis, up)]
    another operation x6 -> x0, other arithmetic: 21.2 us -> none  [conv_valid(): jnp.stack([plane[:, :, offset_y:offset_y + out_y, column_shift:column_shi...]
    concatenate x8 -> x0, local copies, waits for them, and re-layouts: 16.9 us -> none  [extended(): shard = jnp.concatenate([before, shard, after], axis=dim)]
    dot_general x7 -> x0, matrix products: 16.3 us -> none  [the longest x6 15.8 us: conv_valid(): jnp.dot(kernel, patches, preferred_element_type=jnp.float32)]
  transfers between devices with their start and end apart: 12 -> 0, of which waited for: 7 -> 0; matrix products, arithmetic and copies ran while one was open for 12% -> 0% of each run, Pallas kernels for 0% -> 0%
where the time goes in v1:
time: 36.1 us; the launch traced here: 35.9 us
  Pallas kernels  30.2 us (84%)
  local copies, waits for them, and re-layouts  5.07 us (14%)
  between operations  0.69 us (2%)
    pallas_call x1, Pallas kernels, shards(): pl.pallas_call(functools.partial(kernel, n_gz, n_gy), out_shape=(jax.Shap...  30.2 us
    unnamed x13, local copies, waits for them, and re-layouts  3.5 us
    transpose x2, local copies, waits for them, and re-layouts, by_tap(): return jnp.transpose(weight, (2, 1, 3, 0, 4)).reshape(3, 3, 32, 96)  1.24 us

profile of v1, /device:TPU:0, one launch (start us, length us, event | category | flops | bytes accessed | tf_op | source)
XLA Modules:
  0.0 35.9 jit_solution(15136617429270495085)
XLA Ops:
  0.6 0.0 copy-start.4
  0.6 0.7 %copy-done.4 = s32[4,1,1,256]{3,2,1,0:T(1,128)S(1)} copy-done((s32[4,1,1,256]{3,2,1,0:T(1,128)S(1)}, s32[4,1,1,256]{3,2,1,0:T(1,128)}, u32[]{:S(2)}) %copy-start.4) | copy-done | bytes 4120
  1.3 1.1 %copy.10 = bf16[3,3,32,3,32]{4,3,2,1,0:T(4,128)(2,1)S(1)} copy(bf16[3,3,32,3,32]{4,2,0,1,3:T(8,128)(2,1)} %bitcast.10) | data formatting | bytes 110592 | tf_op jit(solution)/shard_map/transpose | solution.py:229
  2.4 0.0 copy-start.3
  2.4 0.2 reshape.19.wt1
  2.6 0.8 %copy-done.3 = bf16[3,3,3,32,32]{4,3,2,1,0:T(8,128)(2,1)S(1)} copy-done((bf16[3,3,3,32,32]{4,3,2,1,0:T(8,128)(2,1)S(1)}, bf16[3,3,3,32,32]{4,3,2,1,0:T(8,128)(2,1)}, u32[]{:S(2)}) %copy-start.3) | copy-done | bytes 55320
  3.3 0.0 copy-start
  3.4 0.2 copy.11
  3.5 0.0 copy-start.1
  3.5 0.0 copy-start.2
  3.5 0.2 reshape.20.wt2
  3.7 0.7 %copy-done = bf16[32,4,8,256]{3,2,1,0:T(8,128)(2,1)S(1)} copy-done((bf16[32,4,8,256]{3,2,1,0:T(8,128)(2,1)S(1)}, bf16[32,4,8,256]{3,2,1,0:T(8,128)(2,1)}, u32[]{:S(2)}) %copy-start) | copy-done | bytes 524312
  4.4 0.0 copy-done.1
  4.4 0.0 copy-done.2
  4.4 30.2 %voxel_contrast.1 = (bf16[32,4,8,256]{3,2,1,0:T(8,128)(2,1)S(1)}, f32[1,256]{1,0:T(1,128)S(1)}) custom-call(bf16[32,4,8,256]{3,2,1,0:T(8,128)(2,1)S(1)} %copy-done, bf16[3,3,32,96]{3,2,1,0:T(8,128)(2,1)S(1)} %reshape.19.wt1, bf16[3,3,32,96]{3,2,1,0:T(8,128)(2,1)S(1)} %reshape.20.wt2, s32[1,256]{1,0:T(1,128)S(1)} %bitcast.8, s32[4,256]{1,0:T(4,128)S(1)} %bitcast.7, ...), custom_call_target="tpu_custom_call" | custom-call | tf_op jit(solution)/shard_map/voxel_contrast/pallas_call | solution.py:235
  34.6 0.8 %copy.17 = bf16[32,4,8,256]{3,2,1,0:T(8,128)(2,1)} copy(bf16[32,4,8,256]{3,2,1,0:T(8,128)(2,1)S(1)} %get-tuple-element.8) | data formatting | bytes 1048576
  35.4 0.6 %copy.18 = f32[1,1,1,256]{3,2,1,0:T(1,128)} copy(f32[1,1,1,256]{3,2,1,0:T(1,128)S(1)} %bitcast.9) | data formatting | bytes 2048
  (1 shorter events, 0.0 us)
Async XLA Ops:
  0.6 0.7 %copy-start.4 = (s32[4,1,1,256]{3,2,1,0:T(1,128)S(1)}, s32[4,1,1,256]{3,2,1,0:T(1,128)}, u32[]{:S(2)}) copy-start(s32[4,1,1,256]{3,2,1,0:T(1,128)} %param.10) | copy-start | bytes 12292
  2.4 0.9 %copy-start.3 = (bf16[3,3,3,32,32]{4,3,2,1,0:T(8,128)(2,1)S(1)}, bf16[3,3,3,32,32]{4,3,2,1,0:T(8,128)(2,1)}, u32[]{:S(2)}) copy-start(bf16[3,3,3,32,32]{4,3,2,1,0:T(8,128)(2,1)} %param.8) | copy-start | bytes 165892
  3.3 1.0 %copy-start = (bf16[32,4,8,256]{3,2,1,0:T(8,128)(2,1)S(1)}, bf16[32,4,8,256]{3,2,1,0:T(8,128)(2,1)}, u32[]{:S(2)}) copy-start(bf16[32,4,8,256]{3,2,1,0:T(8,128)(2,1)} %vol.1) | copy-start | bytes 1572868
  3.5 0.9 %copy-start.1 = (s32[4,4]{1,0:T(4,128)S(1)}, s32[4,4]{1,0:T(4,128)}, u32[]{:S(2)}) copy-start(s32[4,4]{1,0:T(4,128)} %bm.1) | copy-start | bytes 196
  3.5 0.9 %copy-start.2 = (s32[1,1,1,256]{3,2,1,0:T(1,128)S(1)}, s32[1,1,1,256]{3,2,1,0:T(1,128)}, u32[]{:S(2)}) copy-start(s32[1,1,1,256]{3,2,1,0:T(1,128)} %param.9) | copy-start | bytes 3076

commit v2 on v1

v2 whole, which is shorter than its diff:
```python
import functools

import jax
import jax.numpy as jnp
from jax import lax
from jax.experimental import pallas as pl
from jax.experimental.pallas import tpu as pltpu
from jax.sharding import PartitionSpec as P

BF = jnp.bfloat16
F32 = jnp.float32
MESH = pl.DeviceIdType.MESH
DIRS = ((1, 0), (-1, 0), (0, 1), (0, -1), (1, 1), (1, -1), (-1, 1), (-1, -1))
NSEG = 64


def iota(shape, dim):
    return lax.broadcasted_iota(jnp.int32, shape, dim)


def mm(a, b):
    return jnp.dot(a, b, preferred_element_type=F32)


def mm_tn(a, b):
    return lax.dot_general(a, b, (((0,), (0,)), ((), ())), preferred_element_type=F32)


def one_hot(mask):
    return jnp.where(mask, 1.0, 0.0).astype(BF)


def mm_nt(a, b):
    return lax.dot_general(a, b, (((1,), (1,)), ((), ())), preferred_element_type=F32)


def kernel(n_gz, n_gy, vol_hbm, w1_hbm, w2_hbm, sidx_hbm, seg_hbm, bm, feat, loss,
           vol, wts, sidx, seg, xa, xh, xs, xr, q, band, band_halo, part, same, emb_all, acc,
           in_sem, send_sem, recv_sem, xs_sem, xr_sem, es_sem, er_sem):
    gz, gy, gx = lax.axis_index("gz"), lax.axis_index("gy"), lax.axis_index("gx")
    other = 1 - gx

    def inside(dz, dy):
        z, y = gz + dz, gy + dy
        return (z >= 0) & (z < n_gz) & (y >= 0) & (y < n_gy)

    def dev(z, y, x):
        return {"gz": z, "gy": y, "gx": x}

    loads = [
        pltpu.make_async_copy(a, b, in_sem.at[i])
        for i, (a, b) in enumerate((
            (vol_hbm, vol), (w1_hbm, wts.at[0]), (w2_hbm, wts.at[1]), (sidx_hbm, sidx), (seg_hbm, seg)))
    ]
    for load in loads:
        load.start()

    barrier = pltpu.get_barrier_semaphore()
    count = jnp.int32(n_gz)
    pl.semaphore_signal(barrier, inc=1, device_id=dev(gz, gy, other), device_id_type=MESH)
    for off in range(1, n_gz):
        pl.semaphore_signal(barrier, inc=1, device_id=dev(lax.rem(gz + off, n_gz), gy, gx), device_id_type=MESH)
    for dz, dy in DIRS:
        if dy != 0:
            there = inside(dz, dy)
            count = count + there.astype(jnp.int32)

            @pl.when(there)
            def _():
                pl.semaphore_signal(barrier, inc=1, device_id=dev(gz + dz, gy + dy, gx), device_id_type=MESH)

    def target(dz, dy):
        planes = slice(1, 5) if dz == 0 else (slice(0, 1) if dz == 1 else slice(5, 6))
        return planes, slice(0, 32) if dy == 1 else slice(32, 64)

    def halo_copy(r, d):
        dz, dy = DIRS[d]
        to, side = target(dz, dy)
        planes = slice(1, 5) if dz == 0 else (slice(4, 5) if dz == 1 else slice(1, 2))
        if dy == 0:
            src, dst = xa.at[r, planes], xa.at[r, to]
        else:
            src = xa.at[r, planes, slice(224, 256) if dy == 1 else slice(0, 32), :]
            dst = xh.at[r, to, side, :]
        return pltpu.make_async_remote_copy(
            src_ref=src, dst_ref=dst, send_sem=send_sem.at[r, d], recv_sem=recv_sem.at[r, d],
            device_id=dev(gz + dz, gy + dy, gx), device_id_type=MESH)

    def x_copy(r):
        return pltpu.make_async_remote_copy(
            src_ref=xs.at[r], dst_ref=xr.at[r], send_sem=xs_sem.at[r], recv_sem=xr_sem.at[r],
            device_id=dev(gz, gy, other), device_id_type=MESH)

    def picked_dirs(along_z):
        return [(d, dz, dy) for d, (dz, dy) in enumerate(DIRS) if (dz != 0) == along_z]

    def start_halo(r, along_z):
        for d, dz, dy in picked_dirs(along_z):
            @pl.when(inside(dz, dy))
            def _():
                halo_copy(r, d).start()

    def wait_halo(r, along_z):
        for d, dz, dy in picked_dirs(along_z):
            @pl.when(inside(-dz, -dy))
            def _():
                halo_copy(r, d).wait_recv()

    def zero_missing(r):
        for dz, dy in DIRS:
            @pl.when(jnp.logical_not(inside(-dz, -dy)))
            def _():
                to, side = target(dz, dy)
                n = to.stop - to.start
                if dy == 0:
                    xa[r, to] = jnp.zeros((n, 256, 256), BF)
                else:
                    xh[r, to, side, :] = jnp.zeros((n, 32, 256), BF)

    def drain(r):
        for d, (dz, dy) in enumerate(DIRS):
            @pl.when(inside(dz, dy))
            def _():
                halo_copy(r, d).wait_send()
        x_copy(r).wait_send()

    rr, cc = iota((256, 256), 0), iota((256, 256), 1)
    edge_lane = 255 * other

    def build(r):
        place = iota((32, 96), 1) - iota((32, 96), 0)
        wide = jnp.zeros((288, 96), F32)
        for b in range(3):
            wide = wide + mm(wts[r, :, b].reshape(288, 32), one_hot(place == 32 * b))
        wide = wide.astype(BF)
        tap, col = iota((96, 256), 0), iota((96, 256), 1)

        @pl.loop(0, 8)
        def _(y):
            rows = mm(wide, one_hot(tap == col - 32 * y + 32)).astype(BF)
            at = pl.ds(pl.multiple_of(32 * y, 32), 32)
            for a in range(3):
                for c in range(3):
                    n = 32 * (3 * a + c)
                    band[r, c, at, 256 * a:256 * a + 256] = rows[n:n + 32]

        tap, col = iota((96, 192), 0), iota((96, 192), 1)
        low = jnp.zeros((96, 192), F32)
        high = jnp.zeros((96, 192), F32)
        for a in range(3):
            ends = wide[96 * a:96 * a + 96]
            within = (col >> 6) == a
            upper = (col & 32) != 0
            ch = col & 31
            low = low + mm(ends, one_hot(within & jnp.logical_not(upper) & (tap == ch)))
            high = high + mm(ends, one_hot(within & upper & (tap == ch + 64)))
        low, high = low.astype(BF), high.astype(BF)
        for c in range(3):
            band_halo[r, c, 0:32] = low[32 * c:32 * c + 32]
            band_halo[r, c, 32:224] = jnp.zeros((192, 192), BF)
            band_halo[r, c, 224:256] = high[32 * c:32 * c + 32]

    def conv(r, z):
        main = xa[r, pl.ds(z, 3)].reshape(768, 256)
        halo = xh[r, pl.ds(z, 3)].reshape(192, 256)
        p = [mm(band[r, c], main) + mm(band_halo[r, c], halo) for c in range(3)]
        out = p[1] + jnp.where(cc == 0, 0.0, pltpu.roll(p[0], 1, 1))
        part[z] = out + jnp.where(cc == 255, 0.0, pltpu.roll(p[2], 255, 1))

    def send_column(r):
        lanes = iota((16, 256), 1) == edge_lane
        row = iota((16, 256), 0)
        xs[r, :, 0:1536] = mm_nt(one_hot(lanes), xa[r].reshape(1536, 256)).astype(BF)
        ends = jnp.zeros((16, 192), F32)
        for z in range(4):
            ends = ends + mm_nt(one_hot(lanes & (row == z)), xh[r, z:z + 3].reshape(192, 256))
        xs[r, :, 1536:1728] = ends.astype(BF)
        x_copy(r).start()

    def take_column(r):
        x_copy(r).wait_recv()
        row = iota((16, 768), 0)
        col = xr[r, :, 768:1536].astype(F32)
        for z in range(3):
            col = jnp.where(row == z, xr[r, :, 256 * z:256 * z + 768].astype(F32), col)
        side = 2 * other
        q[...] = mm_nt(band[r, side], col.astype(BF)) + mm_nt(band_halo[r, side], xr[r, :, 1536:1728])

    def whole(z):
        col = jnp.sum(jnp.where(iota((256, 16), 1) == z, q[...], 0.0), axis=1, keepdims=True)
        return part[z] + jnp.where(cc == edge_lane, col, 0.0)

    def hide(z):
        xa[1, z + 1] = jnp.maximum(whole(z), 0.0).astype(BF)

    loads[0].wait()
    to_yc = one_hot(cc == (rr & 31) * 8 + (rr >> 5))
    for z in (0, 3, 1, 2):
        xa[0, z + 1] = mm(to_yc, vol[:, z].astype(F32).reshape(256, 256).astype(BF)).astype(BF)
    pl.semaphore_wait(barrier, count)
    start_halo(0, True)
    start_halo(0, False)
    zero_missing(0)
    zero_missing(1)
    for load in loads[1:]:
        load.wait()
    build(0)
    build(1)
    label = iota((NSEG, 256), 0)
    own_seg = one_hot(label == seg[gz])
    for off in range(n_gz):
        block = lax.rem(gz + n_gz - off, n_gz)
        same[off] = mm_tn(one_hot(label == seg[block]), own_seg)
    acc[...] = jnp.zeros((256, 256), F32)
    wait_halo(0, False)
    wait_halo(0, True)
    send_column(0)

    @pl.loop(0, 2)
    def _(i):
        conv(0, 3 * i)

    take_column(0)
    hide(0)
    hide(3)
    start_halo(1, True)

    @pl.loop(1, 3)
    def _(z):
        conv(0, z)
        hide(z)

    start_halo(1, False)
    wait_halo(1, False)

    @pl.loop(1, 3)
    def _(z):
        conv(1, z)

    wait_halo(1, True)
    send_column(1)

    @pl.loop(0, 2)
    def _(i):
        conv(1, 3 * i)

    take_column(1)
    s = sidx[...]
    s_x, s_y, s_z = s & 255, (s >> 8) & 7, s >> 11
    select_x = one_hot(rr == s_x)
    to_cy = one_hot(cc == (rr & 7) * 32 + (rr >> 3))

    @pl.loop(0, 4)
    def _(z):
        f = (whole(z) + xa[0, z + 1].astype(F32)).astype(BF)
        feat[:, z] = mm(to_cy, f).reshape(32, 8, 256).astype(BF)
        acc[...] = jnp.where(s_z == z, mm(f, select_x), acc[...])

    picked = jnp.where((rr >> 5) == s_y, acc[...], 0.0)
    picked = jnp.sum(picked.reshape(8, 32, 256), axis=0)
    norm = jnp.sqrt(jnp.sum(picked * picked, axis=0, keepdims=True) + 1.0)
    emb_all[0] = (picked / norm).astype(BF)

    def emb_copy(off):
        return pltpu.make_async_remote_copy(
            src_ref=emb_all.at[0], dst_ref=emb_all.at[off], send_sem=es_sem.at[off], recv_sem=er_sem.at[off],
            device_id=dev(lax.rem(gz + off, n_gz), gy, gx), device_id_type=MESH)

    for off in range(1, n_gz):
        emb_copy(off).start()
    drain(0)
    drain(1)
    own = emb_all[0]
    total = jnp.zeros((1, 256), F32)
    positive = jnp.zeros((1, 256), F32)
    for off in range(n_gz):
        block = lax.rem(gz + n_gz - off, n_gz)
        if off:
            emb_copy(off).wait_recv()
        e = jnp.exp(mm_tn(emb_all[off], own) * 4.0) * bm[gz, block].astype(F32)
        total = total + jnp.sum(e, axis=0, keepdims=True)
        positive = positive + jnp.sum(e * same[off], axis=0, keepdims=True)
    loss[...] = jnp.log(total) - jnp.log(positive)
    for off in range(1, n_gz):
        emb_copy(off).wait_send()


def shards(n_gz, n_gy, volume, first_weight, second_weight, sample_index, segments, block_match):
    vmem = pl.BlockSpec(memory_space=pltpu.VMEM)
    dma = pltpu.SemaphoreType.DMA
    features, row_loss = pl.pallas_call(
        functools.partial(kernel, n_gz, n_gy),
        out_shape=(
            jax.ShapeDtypeStruct(volume.shape, BF),
            jax.ShapeDtypeStruct((1, 256), F32),
        ),
        in_specs=[pl.BlockSpec(memory_space=pltpu.MemorySpace.HBM)] * 5 + [pl.BlockSpec(memory_space=pltpu.SMEM)],
        out_specs=(vmem, vmem),
        scratch_shapes=[
            pltpu.VMEM(volume.shape, BF),
            pltpu.VMEM((2, 3, 3, 3, 32, 32), BF),
            pltpu.VMEM((1, 256), jnp.int32),
            pltpu.VMEM((n_gz, 1, 256), jnp.int32),
            pltpu.VMEM((2, 6, 256, 256), BF),
            pltpu.VMEM((2, 6, 64, 256), BF),
            pltpu.VMEM((2, 16, 1728), BF),
            pltpu.VMEM((2, 16, 1728), BF),
            pltpu.VMEM((256, 16), F32),
            pltpu.VMEM((2, 3, 256, 768), BF),
            pltpu.VMEM((2, 3, 256, 192), BF),
            pltpu.VMEM((4, 256, 256), F32),
            pltpu.VMEM((n_gz, 256, 256), F32),
            pltpu.VMEM((n_gz, 32, 256), BF),
            pltpu.VMEM((256, 256), F32),
            dma((5,)), dma((2, 8)), dma((2, 8)), dma((2,)), dma((2,)), dma((n_gz,)), dma((n_gz,)),
        ],
        compiler_params=pltpu.CompilerParams(
            collective_id=0, has_side_effects=True, vmem_limit_bytes=40 << 20),
        name="voxel_contrast",
    )(
        volume, first_weight, second_weight, sample_index.reshape(1, 256),
        segments.reshape(segments.shape[0], 1, 256), block_match,
    )
    return features, row_loss.reshape(1, 1, 1, 256)


def solution(mesh):
    in_specs = (
        P(None, ("group", "gz"), "gy", "gx"),
        P(),
        P(),
        P(("group", "gz"), "gy", "gx", None),
        P("group", "gy", "gx", None),
        P("group", None),
    )
    out_specs = (P(None, ("group", "gz"), "gy", "gx"), P(("group", "gz"), "gy", "gx", None))
    body = functools.partial(shards, mesh.shape["gz"], mesh.shape["gy"])
    return jax.shard_map(body, mesh=mesh, in_specs=in_specs, out_specs=out_specs, check_vma=False)
```

time: 36.1 us -> 34.5 us (0.956)
  Pallas kernels: 30.2 us -> 27.9 us
  local copies, waits for them, and re-layouts: 5.07 us -> 5.63 us
    pallas_call x1, Pallas kernels: 30.2 us -> 27.9 us  [shards(): pl.pallas_call(functools.partial(kernel, n_gz, n_gy), out_shape=(jax.Shap...]
    unnamed x13 -> x14, local copies, waits for them, and re-layouts: 3.5 us -> 5.63 us
    transpose x2 -> x0, local copies, waits for them, and re-layouts: 1.24 us -> none  [by_tap(): return jnp.transpose(weight, (2, 1, 3, 0, 4)).reshape(3, 3, 32, 96)]
where the time goes in v2:
time: 34.5 us; the launch traced here: 34.2 us
  Pallas kernels  27.9 us (81%)
  local copies, waits for them, and re-layouts  5.63 us (16%)
  between operations  0.66 us (2%)
    pallas_call x1, Pallas kernels, shards(): pl.pallas_call(functools.partial(kernel, n_gz, n_gy), out_shape=(jax.Shap...  27.9 us
    unnamed x14, local copies, waits for them, and re-layouts  5.63 us

profile of v2, /device:TPU:0, one launch (start us, length us, event | category | flops | bytes accessed | tf_op | source)
XLA Modules:
  0.0 34.2 jit_solution(2284963835709241437)
XLA Ops:
  0.6 0.0 copy-start.4
  0.6 0.0 copy-start.5
  0.7 0.7 %copy-done.4 = s32[4,4]{1,0:T(4,128)S(1)} copy-done((s32[4,4]{1,0:T(4,128)S(1)}, s32[4,4]{1,0:T(4,128)}, u32[]{:S(2)}) %copy-start.4) | copy-done | bytes 88
  1.3 0.0 copy-done.5
  1.3 0.0 copy-start
  1.3 1.0 %copy-done = bf16[32,4,8,256]{3,2,1,0:T(8,128)(2,1)S(1)} copy-done((bf16[32,4,8,256]{3,2,1,0:T(8,128)(2,1)S(1)}, bf16[32,4,8,256]{3,2,1,0:T(8,128)(2,1)}, u32[]{:S(2)}) %copy-start) | copy-done | bytes 524312
  2.4 0.0 copy-start.1
  2.4 0.9 %copy-done.1 = bf16[3,3,3,32,32]{4,3,2,1,0:T(8,128)(2,1)S(1)} copy-done((bf16[3,3,3,32,32]{4,3,2,1,0:T(8,128)(2,1)S(1)}, bf16[3,3,3,32,32]{4,3,2,1,0:T(8,128)(2,1)}, u32[]{:S(2)}) %copy-start.1) | copy-done | bytes 55320
  3.3 0.0 copy-start.2
  3.3 0.9 %copy-done.2 = bf16[3,3,3,32,32]{4,3,2,1,0:T(8,128)(2,1)S(1)} copy-done((bf16[3,3,3,32,32]{4,3,2,1,0:T(8,128)(2,1)S(1)}, bf16[3,3,3,32,32]{4,3,2,1,0:T(8,128)(2,1)}, u32[]{:S(2)}) %copy-start.2) | copy-done | bytes 55320
  4.2 0.0 copy-start.3
  4.2 0.7 %copy-done.3 = s32[4,1,1,256]{3,2,1,0:T(1,128)S(1)} copy-done((s32[4,1,1,256]{3,2,1,0:T(1,128)S(1)}, s32[4,1,1,256]{3,2,1,0:T(1,128)}, u32[]{:S(2)}) %copy-start.3) | copy-done | bytes 4120
  4.9 27.9 %voxel_contrast.1 = (bf16[32,4,8,256]{3,2,1,0:T(8,128)(2,1)S(1)}, f32[1,256]{1,0:T(1,128)S(1)}) custom-call(bf16[32,4,8,256]{3,2,1,0:T(8,128)(2,1)S(1)} %copy-done, bf16[3,3,3,32,32]{4,3,2,1,0:T(8,128)(2,1)S(1)} %copy-done.1, bf16[3,3,3,32,32]{4,3,2,1,0:T(8,128)(2,1)S(1)} %copy-done.2, s32[1,256]{1,0:T(1,128)S(1)} %bitcast.4, s32[4,1,256]{2,1,0:T(1,128)S(1)} %bitcast.3, ...), custom_call_target="tpu_custom_call" | custom-call | tf_op jit(solution)/shard_map/voxel_contrast/pallas_call | solution.py:291
  32.8 0.8 %copy.10 = bf16[32,4,8,256]{3,2,1,0:T(8,128)(2,1)} copy(bf16[32,4,8,256]{3,2,1,0:T(8,128)(2,1)S(1)} %get-tuple-element.8) | data formatting | bytes 1048576
  33.6 0.6 %copy.11 = f32[1,1,1,256]{3,2,1,0:T(1,128)} copy(f32[1,1,1,256]{3,2,1,0:T(1,128)S(1)} %bitcast.5) | data formatting | bytes 2048
Async XLA Ops:
  0.6 0.7 %copy-start.4 = (s32[4,4]{1,0:T(4,128)S(1)}, s32[4,4]{1,0:T(4,128)}, u32[]{:S(2)}) copy-start(s32[4,4]{1,0:T(4,128)} %bm.1) | copy-start | bytes 196
  0.6 0.7 %copy-start.5 = (s32[1,1,1,256]{3,2,1,0:T(1,128)S(1)}, s32[1,1,1,256]{3,2,1,0:T(1,128)}, u32[]{:S(2)}) copy-start(s32[1,1,1,256]{3,2,1,0:T(1,128)} %param.9) | copy-start | bytes 3076
  1.3 1.0 %copy-start = (bf16[32,4,8,256]{3,2,1,0:T(8,128)(2,1)S(1)}, bf16[32,4,8,256]{3,2,1,0:T(8,128)(2,1)}, u32[]{:S(2)}) copy-start(bf16[32,4,8,256]{3,2,1,0:T(8,128)(2,1)} %vol_hbm.1) | copy-start | bytes 1572868
  2.4 0.9 %copy-start.1 = (bf16[3,3,3,32,32]{4,3,2,1,0:T(8,128)(2,1)S(1)}, bf16[3,3,3,32,32]{4,3,2,1,0:T(8,128)(2,1)}, u32[]{:S(2)}) copy-start(bf16[3,3,3,32,32]{4,3,2,1,0:T(8,128)(2,1)} %w1_hbm.1) | copy-start | bytes 165892
  3.3 0.9 %copy-start.2 = (bf16[3,3,3,32,32]{4,3,2,1,0:T(8,128)(2,1)S(1)}, bf16[3,3,3,32,32]{4,3,2,1,0:T(8,128)(2,1)}, u32[]{:S(2)}) copy-start(bf16[3,3,3,32,32]{4,3,2,1,0:T(8,128)(2,1)} %w2_hbm.1) | copy-start | bytes 165892
  4.2 0.7 %copy-start.3 = (s32[4,1,1,256]{3,2,1,0:T(1,128)S(1)}, s32[4,1,1,256]{3,2,1,0:T(1,128)}, u32[]{:S(2)}) copy-start(s32[4,1,1,256]{3,2,1,0:T(1,128)} %param.10) | copy-start | bytes 12292

commit v3 on v2

--- a/solution.py
+++ b/solution.py
@@ -315,7 +315,7 @@
             dma((5,)), dma((2, 8)), dma((2, 8)), dma((2,)), dma((2,)), dma((n_gz,)), dma((n_gz,)),
         ],
         compiler_params=pltpu.CompilerParams(
-            collective_id=0, has_side_effects=True, vmem_limit_bytes=40 << 20),
+            collective_id=0, has_side_effects=True, vmem_limit_bytes=56 << 20),
         name="voxel_contrast",
     )(
         volume, first_weight, second_weight, sample_index.reshape(1, 256),

time: 34.5 us -> 31.5 us (0.913)
  local copies, waits for them, and re-layouts: 5.63 us -> 2.44 us
    unnamed x14 -> x4, local copies, waits for them, and re-layouts: 5.63 us -> 2.44 us
where the time goes in v3:
time: 31.5 us; the launch traced here: 31.3 us
  Pallas kernels  28.2 us (90%)
  local copies, waits for them, and re-layouts  2.44 us (8%)
  between operations  0.65 us (2%)
    pallas_call x1, Pallas kernels, shards(): pl.pallas_call(functools.partial(kernel, n_gz, n_gy), out_shape=(jax.Shap...  28.2 us
    unnamed x4, local copies, waits for them, and re-layouts  2.44 us

profile of v3, /device:TPU:0, one launch (start us, length us, event | category | flops | bytes accessed | tf_op | source)
XLA Modules:
  0.0 31.3 jit_solution(3466011157857476583)
XLA Ops:
  0.6 28.2 %voxel_contrast.1 = (bf16[32,4,8,256]{3,2,1,0:T(8,128)(2,1)}, f32[1,256]{1,0:T(1,128)}) custom-call(bf16[32,4,8,256]{3,2,1,0:T(8,128)(2,1)} %vol_hbm.1, bf16[3,3,3,32,32]{4,3,2,1,0:T(8,128)(2,1)} %w1_hbm.1, bf16[3,3,3,32,32]{4,3,2,1,0:T(8,128)(2,1)} %w2_hbm.1, s32[1,256]{1,0:T(1,128)} %bitcast.4, s32[4,1,256]{2,1,0:T(1,128)} %bitcast.3, s32[4,4]{1,0:T(4,128)} %bm.1), custom_call_target="tpu_custom_call" | custom-call | tf_op jit(solution)/shard_map/voxel_contrast/pallas_call | solution.py:291
  28.8 0.0 copy-start
  28.9 1.9 %copy.10 = bf16[32,4,8,256]{3,2,1,0:T(8,128)(2,1)} copy(bf16[32,4,8,256]{3,2,1,0:T(8,128)(2,1)} %get-tuple-element.8) | data formatting | bytes 1048576
  30.7 0.0 copy-done
  30.7 0.6 %copy.11 = f32[1,1,1,256]{3,2,1,0:T(1,128)} copy(f32[1,1,1,256]{3,2,1,0:T(1,128)S(1)} %bitcast.5) | data formatting | bytes 2048
Async XLA Ops:
  28.8 1.9 %copy-start = (f32[1,256]{1,0:T(1,128)S(1)}, f32[1,256]{1,0:T(1,128)}, u32[]{:S(2)}) copy-start(f32[1,256]{1,0:T(1,128)} %get-tuple-element.5) | copy-start | bytes 3076

commit v4 on v2

--- a/solution.py
+++ b/solution.py
@@ -10,7 +10,8 @@
 BF = jnp.bfloat16
 F32 = jnp.float32
 MESH = pl.DeviceIdType.MESH
-DIRS = ((1, 0), (-1, 0), (0, 1), (0, -1), (1, 1), (1, -1), (-1, 1), (-1, -1))
+DIRS = ((1, 0), (-1, 0), (0, 1), (0, -1), (1, 1), (1, -1), (-1, 1), (-1, -1)) + ((1, 0), (-1, 0)) * 3
+FACE_ROWS = 64
 NSEG = 64
 
 
@@ -34,8 +35,8 @@
     return lax.dot_general(a, b, (((1,), (1,)), ((), ())), preferred_element_type=F32)
 
 
-def kernel(n_gz, n_gy, vol_hbm, w1_hbm, w2_hbm, sidx_hbm, seg_hbm, bm, feat, loss,
-           vol, wts, sidx, seg, xa, xh, xs, xr, q, band, band_halo, part, same, emb_all, acc,
+def kernel(n_gz, n_gy, vol_hbm, w1_hbm, w2_hbm, sidx_hbm, seg_hbm, bm_hbm, feat, loss,
+           vol, wts, sidx, seg, bm, xa, xh, xs, xr, q, band, band_halo, part, made, same, emb_all, acc,
            in_sem, send_sem, recv_sem, xs_sem, xr_sem, es_sem, er_sem):
     gz, gy, gx = lax.axis_index("gz"), lax.axis_index("gy"), lax.axis_index("gx")
     other = 1 - gx
@@ -50,7 +51,8 @@
     loads = [
         pltpu.make_async_copy(a, b, in_sem.at[i])
         for i, (a, b) in enumerate((
-            (vol_hbm, vol), (w1_hbm, wts.at[0]), (w2_hbm, wts.at[1]), (sidx_hbm, sidx), (seg_hbm, seg)))
+            (vol_hbm, vol), (w1_hbm, wts.at[0]), (w2_hbm, wts.at[1]), (sidx_hbm, sidx), (seg_hbm, seg),
+            (bm_hbm, bm)))
     ]
     for load in loads:
         load.start()
@@ -78,7 +80,9 @@
         to, side = target(dz, dy)
         planes = slice(1, 5) if dz == 0 else (slice(4, 5) if dz == 1 else slice(1, 2))
         if dy == 0:
-            src, dst = xa.at[r, planes], xa.at[r, to]
+            first = FACE_ROWS * (0 if d < 8 else d // 2 - 3)
+            rows = slice(first, first + FACE_ROWS)
+            src, dst = xa.at[r, planes, rows, :], xa.at[r, to, rows, :]
         else:
             src = xa.at[r, planes, slice(224, 256) if dy == 1 else slice(0, 32), :]
             dst = xh.at[r, to, side, :]
@@ -107,7 +111,7 @@
                 halo_copy(r, d).wait_recv()
 
     def zero_missing(r):
-        for dz, dy in DIRS:
+        for dz, dy in DIRS[:8]:
             @pl.when(jnp.logical_not(inside(-dz, -dy)))
             def _():
                 to, side = target(dz, dy)
@@ -253,7 +257,7 @@
     @pl.loop(0, 4)
     def _(z):
         f = (whole(z) + xa[0, z + 1].astype(F32)).astype(BF)
-        feat[:, z] = mm(to_cy, f).reshape(32, 8, 256).astype(BF)
+        made[z] = f
         acc[...] = jnp.where(s_z == z, mm(f, select_x), acc[...])
 
     picked = jnp.where((rr >> 5) == s_y, acc[...], 0.0)
@@ -268,8 +272,11 @@
 
     for off in range(1, n_gz):
         emb_copy(off).start()
-    drain(0)
-    drain(1)
+
+    @pl.loop(0, 4)
+    def _(z):
+        feat[:, z] = mm(to_cy, made[z]).reshape(32, 8, 256).astype(BF)
+
     own = emb_all[0]
     total = jnp.zeros((1, 256), F32)
     positive = jnp.zeros((1, 256), F32)
@@ -283,6 +290,8 @@
     loss[...] = jnp.log(total) - jnp.log(positive)
     for off in range(1, n_gz):
         emb_copy(off).wait_send()
+    drain(0)
+    drain(1)
 
 
 def shards(n_gz, n_gy, volume, first_weight, second_weight, sample_index, segments, block_match):
@@ -294,13 +303,14 @@
             jax.ShapeDtypeStruct(volume.shape, BF),
             jax.ShapeDtypeStruct((1, 256), F32),
         ),
-        in_specs=[pl.BlockSpec(memory_space=pltpu.MemorySpace.HBM)] * 5 + [pl.BlockSpec(memory_space=pltpu.SMEM)],
+        in_specs=[pl.BlockSpec(memory_space=pltpu.MemorySpace.HBM)] * 6,
         out_specs=(vmem, vmem),
         scratch_shapes=[
             pltpu.VMEM(volume.shape, BF),
             pltpu.VMEM((2, 3, 3, 3, 32, 32), BF),
             pltpu.VMEM((1, 256), jnp.int32),
             pltpu.VMEM((n_gz, 1, 256), jnp.int32),
+            pltpu.SMEM(block_match.shape, jnp.int32),
             pltpu.VMEM((2, 6, 256, 256), BF),
             pltpu.VMEM((2, 6, 64, 256), BF),
             pltpu.VMEM((2, 16, 1728), BF),
@@ -309,17 +319,19 @@
             pltpu.VMEM((2, 3, 256, 768), BF),
             pltpu.VMEM((2, 3, 256, 192), BF),
             pltpu.VMEM((4, 256, 256), F32),
+            pltpu.VMEM((4, 256, 256), BF),
             pltpu.VMEM((n_gz, 256, 256), F32),
             pltpu.VMEM((n_gz, 32, 256), BF),
             pltpu.VMEM((256, 256), F32),
-            dma((5,)), dma((2, 8)), dma((2, 8)), dma((2,)), dma((2,)), dma((n_gz,)), dma((n_gz,)),
+            dma((6,)), dma((2, len(DIRS))), dma((2, len(DIRS))), dma((2,)), dma((2,)), dma((n_gz,)), dma((n_gz,)),
         ],
         compiler_params=pltpu.CompilerParams(
             collective_id=0, has_side_effects=True, vmem_limit_bytes=40 << 20),
         name="voxel_contrast",
     )(
-        volume, first_weight, second_weight, sample_index.reshape(1, 256),
-        segments.reshape(segments.shape[0], 1, 256), block_match,
+        *(pltpu.with_memory_space_constraint(a, pltpu.MemorySpace.HBM) for a in (
+            volume, first_weight, second_weight, sample_index.reshape(1, 256),
+            segments.reshape(segments.shape[0], 1, 256), block_match)),
     )
     return features, row_loss.reshape(1, 1, 1, 256)
 

time: 34.5 us -> 28.2 us (0.82)
  local copies, waits for them, and re-layouts: 5.63 us -> 1.36 us
  Pallas kernels: 27.9 us -> 26 us
    unnamed x14 -> x2, local copies, waits for them, and re-layouts: 5.63 us -> 1.36 us
    pallas_call x1, Pallas kernels: 27.9 us -> 26 us  [shards(): pl.pallas_call(functools.partial(kernel, n_gz, n_gy), out_shape=(jax.Shap...]
where the time goes in v4:
time: 28.2 us; the launch traced here: 28 us
  Pallas kernels  26 us (92%)
  local copies, waits for them, and re-layouts  1.36 us (5%)
  between operations  0.64 us (2%)
    pallas_call x1, Pallas kernels, shards(): pl.pallas_call(functools.partial(kernel, n_gz, n_gy), out_shape=(jax.Shap...  26 us
    unnamed x2, local copies, waits for them, and re-layouts  1.36 us

profile of v4, /device:TPU:0, one launch (start us, length us, event | category | flops | bytes accessed | tf_op | source)
XLA Modules:
  0.0 28.0 jit_solution(10768877386841296405)
XLA Ops:
  0.6 26.0 %voxel_contrast.1 = (bf16[32,4,8,256]{3,2,1,0:T(8,128)(2,1)S(1)}, f32[1,256]{1,0:T(1,128)S(1)}) custom-call(bf16[32,4,8,256]{3,2,1,0:T(8,128)(2,1)} %vol_hbm.1, bf16[3,3,3,32,32]{4,3,2,1,0:T(8,128)(2,1)} %w1_hbm.1, bf16[3,3,3,32,32]{4,3,2,1,0:T(8,128)(2,1)} %w2_hbm.1, s32[1,256]{1,0:T(1,128)} %bitcast.5, s32[4,1,256]{2,1,0:T(1,128)} %bitcast.4, s32[4,4]{1,0:T(4,128)} %bm_hbm.1), custom_call_target="tpu_custom_call" | custom-call | tf_op jit(solution)/shard_map/voxel_contrast/pallas_call | solution.py:300
  26.7 0.8 %copy.10 = bf16[32,4,8,256]{3,2,1,0:T(8,128)(2,1)} copy(bf16[32,4,8,256]{3,2,1,0:T(8,128)(2,1)S(1)} %get-tuple-element.8) | data formatting | bytes 1048576
  27.5 0.6 %copy.11 = f32[1,1,1,256]{3,2,1,0:T(1,128)} copy(f32[1,1,1,256]{3,2,1,0:T(1,128)S(1)} %bitcast.3) | data formatting | bytes 2048

commit v5 on v4

--- a/solution.py
+++ b/solution.py
@@ -209,7 +209,6 @@
     for load in loads[1:]:
         load.wait()
     build(0)
-    build(1)
     label = iota((NSEG, 256), 0)
     own_seg = one_hot(label == seg[gz])
     for off in range(n_gz):
@@ -217,6 +216,11 @@
         same[off] = mm_tn(one_hot(label == seg[block]), own_seg)
     acc[...] = jnp.zeros((256, 256), F32)
     wait_halo(0, False)
+
+    @pl.loop(1, 3)
+    def _(z):
+        conv(0, z)
+
     wait_halo(0, True)
     send_column(0)
 
@@ -229,12 +233,10 @@
     hide(3)
     start_halo(1, True)
 
-    @pl.loop(1, 3)
-    def _(z):
-        conv(0, z)
-        hide(z)
-
+    hide(1)
+    hide(2)
     start_halo(1, False)
+    build(1)
     wait_halo(1, False)
 
     @pl.loop(1, 3)

time: 28.2 us -> 27.2 us (0.965)
  Pallas kernels: 26 us -> 25.1 us
    pallas_call x1, Pallas kernels: 26 us -> 25.1 us  [shards(): pl.pallas_call(functools.partial(kernel, n_gz, n_gy), out_shape=(jax.Shap...]
where the time goes in v5:
time: 27.2 us; the launch traced here: 27.1 us
  Pallas kernels  25.1 us (92%)
  local copies, waits for them, and re-layouts  1.36 us (5%)
  between operations  0.64 us (2%)
    pallas_call x1, Pallas kernels, shards(): pl.pallas_call(functools.partial(kernel, n_gz, n_gy), out_shape=(jax.Shap...  25.1 us
    unnamed x2, local copies, waits for them, and re-layouts  1.36 us

profile of v5, /device:TPU:0, one launch (start us, length us, event | category | flops | bytes accessed | tf_op | source)
XLA Modules:
  0.0 27.1 jit_solution(14875840627807401703)
XLA Ops:
  0.6 25.1 %voxel_contrast.1 = (bf16[32,4,8,256]{3,2,1,0:T(8,128)(2,1)S(1)}, f32[1,256]{1,0:T(1,128)S(1)}) custom-call(bf16[32,4,8,256]{3,2,1,0:T(8,128)(2,1)} %vol_hbm.1, bf16[3,3,3,32,32]{4,3,2,1,0:T(8,128)(2,1)} %w1_hbm.1, bf16[3,3,3,32,32]{4,3,2,1,0:T(8,128)(2,1)} %w2_hbm.1, s32[1,256]{1,0:T(1,128)} %bitcast.5, s32[4,1,256]{2,1,0:T(1,128)} %bitcast.4, s32[4,4]{1,0:T(4,128)} %bm_hbm.1), custom_call_target="tpu_custom_call" | custom-call | tf_op jit(solution)/shard_map/voxel_contrast/pallas_call | solution.py:302
  25.7 0.8 %copy.10 = bf16[32,4,8,256]{3,2,1,0:T(8,128)(2,1)} copy(bf16[32,4,8,256]{3,2,1,0:T(8,128)(2,1)S(1)} %get-tuple-element.8) | data formatting | bytes 1048576
  26.5 0.6 %copy.11 = f32[1,1,1,256]{3,2,1,0:T(1,128)} copy(f32[1,1,1,256]{3,2,1,0:T(1,128)S(1)} %bitcast.3) | data formatting | bytes 2048
